TPU v7x, 256 devices: a whole 4x4x8 slice. The times are simulated.
256 devices in a mesh: dp: 8 (over z), space: 32 (over x, y, core).
Axes of the slice: x: 4, y: 4, z: 8, core: 2. Of those that a mesh axis runs over, the one named last changes fastest.
Arguments:
- lateral3: bfloat16 [32, 128, 128, 256], P('dp', 'space'), may hold values from -1200 to 1200
- lateral4: bfloat16 [32, 64, 64, 256], P('dp', 'space'), may hold values from -1200 to 1200
- lateral5: bfloat16 [32, 32, 32, 256], P('dp', 'space'), may hold values from -1200 to 1200
- conv_weight3: bfloat16 [3, 3, 256, 256], P(None, None, None, ('dp', 'space')), may hold values from -0.125 to 0.125
- conv_weight4: bfloat16 [3, 3, 256, 256], P(None, None, None, ('dp', 'space')), may hold values from -0.125 to 0.125
- conv_weight5: bfloat16 [3, 3, 256, 256], P(None, None, None, ('dp', 'space')), may hold values from -0.125 to 0.125
- norm_gain3: float32 [256], replicated, may hold values from 0.1 to 1.9
- norm_shift3: float32 [256], replicated, may hold values from -3 to 3
- norm_gain4: float32 [256], replicated, may hold values from 0.1 to 1.9
- norm_shift4: float32 [256], replicated, may hold values from -3 to 3
- norm_gain5: float32 [256], replicated, may hold values from 0.1 to 1.9
- norm_shift5: float32 [256], replicated, may hold values from -3 to 3
Outputs:
- pyramid3: float32 [32, 128, 128, 256], P('dp', 'space')
- pyramid4: float32 [32, 64, 64, 256], P('dp', 'space')
- pyramid5: float32 [32, 32, 32, 256], P('dp', 'space')
All inputs are finite; a program needn't handle non-finite values.
Results may differ from a plain program's by a relative error of at most 0.007.
Values may be sent and summed in bfloat16 or wider, within the bound.
A program may use at most 64 MiB of HBM per device.

v0:
```python
import jax
import jax.numpy as jnp
from jax import lax
from jax.sharding import Mesh
from jax.sharding import PartitionSpec as P

G = 32
SPACE = ("space_0", "space_1", "space_2")
DP_SPACE = ("dp", "space_0", "space_1", "space_2")


epsilon = 1e-05


def sent_to_all(array, axis):
    devices = lax.axis_size(axis)
    return lax.all_to_all(
        jnp.broadcast_to(array[None], (devices, *array.shape)), axis, 0, 0, tiled=True
    )


def taken_together(array, axis):
    everything = sent_to_all(array, axis)
    return jnp.sum(everything, axis=0)


def extended(array, sides, width):
    for axis, dim in sides:
        devices, length = (lax.axis_size(axis), array.shape[dim])
        up = [(i, (i + 1) % devices) for i in range(devices - 1)]
        down = [(j, i) for i, j in up]
        last = lax.slice_in_dim(array, length - width, length, axis=dim)
        first = lax.slice_in_dim(array, 0, width, axis=dim)
        before = lax.ppermute(last, axis, up)
        after = lax.ppermute(first, axis, down)
        array = jnp.concatenate([before, array, after], axis=dim)
    return array


def in_order(blocks, dim):
    blocks = jnp.moveaxis(blocks, 0, dim)
    shape = blocks.shape
    return blocks.reshape(*shape[:dim], shape[dim] * shape[dim + 1], *shape[dim + 2 :])


def gather_axes(array, axes, dim):
    far, near = axes
    first = sent_to_all(array, far)
    blocks = jnp.swapaxes(sent_to_all(first, near), 0, 1)
    return in_order(blocks.reshape(-1, *array.shape), dim)


def enlarge(values):
    return jnp.repeat(jnp.repeat(values, 2, axis=1), 2, axis=2)


def convolve(padded, kernel, margin):
    return lax.conv_general_dilated(
        padded,
        kernel,
        (1, 1),
        (margin, (1, 1)),
        dimension_numbers=("NHWC", "HWIO", "NHWC"),
        preferred_element_type=jnp.float32,
    )


def rowwise(padded, kernel_piece):
    return convolve(padded, kernel_piece, (0, 0))


def grouped(values, groups):
    return values.reshape(
        values.shape[0], values.shape[1], values.shape[2], groups, values.shape[3] // groups
    )


def raw_moments(values, groups):
    blocks = grouped(values, groups)
    return jnp.stack([jnp.sum(blocks, axis=(1, 2, 4)), jnp.sum(blocks * blocks, axis=(1, 2, 4))])


def derive_raw(paired, volume):
    center = paired[0] / volume
    spread = jnp.maximum(paired[1] / volume - center * center, 0.0)
    return (center, spread)


def normalize(values, center, spread, gain_vector, shift_vector, groups):
    deviation = grouped(values, groups) - center[:, None, None, :, None]
    scaled = deviation * lax.rsqrt(spread + epsilon)[:, None, None, :, None]
    return scaled.reshape(values.shape) * gain_vector + shift_vector


def norm_levels(levels):
    strip_count = lax.axis_size(SPACE)
    volumes = [
        record[0].shape[1] * strip_count * record[0].shape[2] * (record[0].shape[3] // G)
        for record in levels
    ]
    packed = taken_together(
        jnp.concatenate([raw_moments(record[0], G) for record in levels], axis=0), SPACE
    )
    statistics = [
        derive_raw(packed[2 * number : 2 * number + 2], volumes[number])
        for number in range(len(levels))
    ]
    return [
        normalize(record[0], stats_pair[0], stats_pair[1], record[1], record[2], G)
        for record, stats_pair in zip(levels, statistics)
    ]


def local(
    lateral3,
    lateral4,
    lateral5,
    conv_weight3,
    conv_weight4,
    conv_weight5,
    norm_gain3,
    norm_shift3,
    norm_gain4,
    norm_shift4,
    norm_gain5,
    norm_shift5,
):
    merged4 = (lateral4.astype(jnp.float32) + enlarge(lateral5).astype(jnp.float32)).astype(
        jnp.bfloat16
    )
    padded4 = extended(merged4, ((SPACE, 1),), 1)
    merged3 = (lateral3.astype(jnp.float32) + enlarge(merged4).astype(jnp.float32)).astype(
        jnp.bfloat16
    )
    padded3 = extended(merged3, ((SPACE, 1),), 1)
    filtered3 = rowwise(
        padded3, gather_axes(conv_weight3, (("dp", "space_0"), ("space_1", "space_2")), 3)
    )
    filtered4 = rowwise(
        padded4, gather_axes(conv_weight4, (("dp", "space_0"), ("space_1", "space_2")), 3)
    )
    levels = [(filtered3, norm_gain3, norm_shift3), (filtered4, norm_gain4, norm_shift4)]
    padded5 = extended(lateral5, ((SPACE, 1),), 1)
    filtered5 = rowwise(
        padded5, gather_axes(conv_weight5, (("dp", "space_0"), ("space_1", "space_2")), 3)
    )
    levels.append((filtered5, norm_gain5, norm_shift5))
    results = norm_levels(levels)
    pyramid3 = results[0]
    pyramid4 = results[1]
    pyramid5 = results[2]
    return (pyramid3, pyramid4, pyramid5)


def solution(mesh):
    torus = Mesh(
        mesh.devices.reshape(mesh.shape["dp"], 4, 4, 2), ("dp", "space_0", "space_1", "space_2")
    )
    return jax.shard_map(
        local,
        mesh=torus,
        in_specs=(
            P("dp", SPACE, None, None),
            P("dp", SPACE, None, None),
            P("dp", SPACE, None, None),
            P(None, None, None, DP_SPACE),
            P(None, None, None, DP_SPACE),
            P(None, None, None, DP_SPACE),
            P(),
            P(),
            P(),
            P(),
            P(),
            P(),
        ),
        out_specs=(
            P("dp", SPACE, None, None),
            P("dp", SPACE, None, None),
            P("dp", SPACE, None, None),
        ),
        check_vma=False,
    )
```

profile of v0, /device:TPU:1, one launch (start us, length us, event | category | flops | bytes accessed | tf_op | source)
XLA Modules:
  0.0 169.6 jit_solution(16272046771749662667)
XLA Ops:
  1.4 21.7 %all_to_all.35 = bf16[32,3,3,256,1]{3,2,1,4,0:T(4,128)(2,1)} all-to-all(bf16[32,3,3,256,1]{3,2,1,4,0:T(4,128)(2,1)S(1)} %broadcast_in_dim.39), channel_id=1, replica_groups=mesh['dp'=8,'space_0'=4,'space_1'=4,'space_2'=2] {'dp','space_0'}, dimensions={0} | all-to-all | bytes 294912 | tf_op jit(solution)/shard_map/all_to_all | solution.py:17
  23.9 14.3 %all_to_all.36 = bf16[32,3,3,256,1]{3,2,1,4,0:T(4,128)(2,1)S(1)} all-to-all(bf16[32,3,3,256,1]{3,2,1,4,0:T(4,128)(2,1)S(1)} %broadcast_in_dim.91), channel_id=1, replica_groups=mesh['dp'=8,'space_0'=4,'space_1'=4,'space_2'=2] {'dp','space_0'}, dimensions={0} | all-to-all | bytes 294912 | tf_op jit(solution)/shard_map/all_to_all | solution.py:17
  38.1 1.4 broadcast_in_dim.43
  39.6 3.9 %all-to-all-start.2 = ((bf16[32,3,3,256,1]{3,2,1,4,0:T(4,128)(2,1)}), bf16[32,3,3,256,1]{3,2,1,4,0:T(4,128)(2,1)S(1)}, u32[]{:S(2)}, u32[]{:S(2)}) async-start(bf16[32,3,3,256,1]{3,2,1,4,0:T(4,128)(2,1)} %broadcast_in_dim.43), calls=%async_computation.2 | async-start | bytes 393216 | tf_op jit(solution)/shard_map/all_to_all | solution.py:17
  43.4 6.2 %collective-permute-start.4 = (bf16[4,1,32,256]{3,2,1,0:T(8,128)(2,1)}, bf16[4,1,32,256]{3,2,1,0:T(8,128)(2,1)}, u32[]{:S(2)}, u32[]{:S(2)}) collective-permute-start(bf16[4,1,32,256]{3,2,1,0:T(8,128)(2,1)} %param.14), channel_id=1, source_target_pairs={{0,1},{1,2},{2,3},{3,4},{4,5},{5,6},{6,7},{7,8},{8,9},{9,10},{10,1... | collective-permute-start | bytes 196616 | tf_op jit(solution)/shard_map/ppermute | solution.py:34
  49.7 1.9 %collective-permute-start.5 = (bf16[4,1,32,256]{3,2,1,0:T(8,128)(2,1)}, bf16[4,1,32,256]{3,2,1,0:T(8,128)(2,1)}, u32[]{:S(2)}, u32[]{:S(2)}) collective-permute-start(bf16[4,1,32,256]{3,2,1,0:T(8,128)(2,1)} %param.14), channel_id=1, source_target_pairs={{1,0},{2,1},{3,2},{4,3},{5,4},{6,5},{7,6},{8,7},{9,8},{10,9},{11,1... | collective-permute-start | bytes 196616 | tf_op jit(solution)/shard_map/ppermute | solution.py:35
  51.7 1.8 %all-to-all-done.2 = bf16[32,3,3,256,1]{3,2,1,4,0:T(4,128)(2,1)S(1)} async-done(((bf16[32,3,3,256,1]{3,2,1,4,0:T(4,128)(2,1)}), bf16[32,3,3,256,1]{3,2,1,4,0:T(4,128)(2,1)S(1)}, u32[]{:S(2)}, u32[]{:S(2)}) %all-to-all-start.2) | async-done | bytes 147488 | tf_op jit(solution)/shard_map/all_to_all | solution.py:17
  54.6 8.9 %all-to-all-start.5 = ((bf16[8,32,3,3,256,1]{4,1,3,2,5,0:T(8,128)(2,1)}), bf16[8,32,3,3,256,1]{4,1,3,2,5,0:T(8,128)(2,1)S(1)}, u32[]{:S(2)}, u32[]{:S(2)}) async-start(bf16[8,32,3,3,256,1]{4,1,3,2,5,0:T(8,128)(2,1)} %broadcast_in_dim.93), calls=%async_computation.5 | async-start | bytes 2359296 | tf_op jit(solution)/shard_map/all_to_all | solution.py:17
  64.6 3.5 %collective-permute-start.2 = (bf16[4,1,64,256]{3,2,1,0:T(8,128)(2,1)}, bf16[4,1,64,256]{3,2,1,0:T(8,128)(2,1)}, u32[]{:S(2)}, u32[]{:S(2)}) collective-permute-start(bf16[4,1,64,256]{3,2,1,0:T(8,128)(2,1)} %get-tuple-element.17), channel_id=1, source_target_pairs={{0,1},{1,2},{2,3},{3,4},{4,5},{5,6},{6,7},{7,8},{8,9},{9,10},{10,1... | collective-permute-start | bytes 393224 | tf_op jit(solution)/shard_map/ppermute | solution.py:34
  68.1 1.9 %collective-permute-start.3 = (bf16[4,1,64,256]{3,2,1,0:T(8,128)(2,1)}, bf16[4,1,64,256]{3,2,1,0:T(8,128)(2,1)}, u32[]{:S(2)}, u32[]{:S(2)}) collective-permute-start(bf16[4,1,64,256]{3,2,1,0:T(8,128)(2,1)} %get-tuple-element.18), channel_id=1, source_target_pairs={{1,0},{2,1},{3,2},{4,3},{5,4},{6,5},{7,6},{8,7},{9,8},{10,9},{11,1... | collective-permute-start | bytes 393224 | tf_op jit(solution)/shard_map/ppermute | solution.py:35
  70.9 2.4 %convert_element_type.42 = f32[4,4,128,256]{3,2,1,0:T(8,128)} reshape(f32[4,4,64,2,256]{4,3,2,1,0:T(2,128)S(1)} %broadcast_in_dim.37) | data formatting | bytes 4194304 | tf_op jit(solution)/shard_map/convert_element_type | solution.py:132
  73.3 2.2 %add_convert_fusion = bf16[4,4,128,256]{3,2,1,0:T(8,128)(2,1)S(1)} fusion(f32[4,4,128,256]{3,2,1,0:T(8,128)} %convert_element_type.42, bf16[4,4,128,256]{3,2,1,0:T(8,128)(2,1)} %param.12), kind=kLoop, calls=%fused_computation.9 | loop fusion | flops 1572864 | bytes 4194304 | tf_op jit(solution)/shard_map/convert_element_type | solution.py:132
  75.6 4.3 %all-to-all-done.5 = bf16[8,32,3,3,256,1]{4,1,3,2,5,0:T(8,128)(2,1)S(1)} async-done(((bf16[8,32,3,3,256,1]{4,1,3,2,5,0:T(8,128)(2,1)}), bf16[8,32,3,3,256,1]{4,1,3,2,5,0:T(8,128)(2,1)S(1)}, u32[]{:S(2)}, u32[]{:S(2)}) %all-to-all-start.5) | async-done | bytes 1179680 | tf_op jit(solution)/shard_map/all_to_all | solution.py:17
  81.1 5.8 %all-to-all-start.3 = ((bf16[8,32,3,3,256,1]{4,1,3,2,5,0:T(8,128)(2,1)}), bf16[8,32,3,3,256,1]{4,1,3,2,5,0:T(8,128)(2,1)}, u32[]{:S(2)}, u32[]{:S(2)}) async-start(bf16[8,32,3,3,256,1]{4,1,3,2,5,0:T(8,128)(2,1)} %broadcast_in_dim.89), calls=%async_computation.3 | async-start | bytes 2359296 | tf_op jit(solution)/shard_map/all_to_all | solution.py:17
  86.9 3.5 %collective-permute-start = (bf16[4,1,128,256]{3,2,1,0:T(8,128)(2,1)S(1)}, bf16[4,1,128,256]{3,2,1,0:T(8,128)(2,1)S(1)}, u32[]{:S(2)}, u32[]{:S(2)}) collective-permute-start(bf16[4,1,128,256]{3,2,1,0:T(8,128)(2,1)S(1)} %get-tuple-element.15), channel_id=1, source_target_pairs={{0,1},{1,2},{2,3},{3,4},{4,5},{5,6},{6,7},{7,8},{8,9},{9,10},{10,1... | collective-permute-start | bytes 786440 | tf_op jit(solution)/shard_map/ppermute | solution.py:34
  90.5 1.9 %collective-permute-start.1 = (bf16[4,1,128,256]{3,2,1,0:T(8,128)(2,1)S(1)}, bf16[4,1,128,256]{3,2,1,0:T(8,128)(2,1)S(1)}, u32[]{:S(2)}, u32[]{:S(2)}) collective-permute-start(bf16[4,1,128,256]{3,2,1,0:T(8,128)(2,1)S(1)} %get-tuple-element.16), channel_id=1, source_target_pairs={{1,0},{2,1},{3,2},{4,3},{5,4},{6,5},{7,6},{8,7},{9,8},{10,9},{11,1... | collective-permute-start | bytes 786440 | tf_op jit(solution)/shard_map/ppermute | solution.py:35
  97.4 5.7 %collective-permute-done = bf16[4,1,128,256]{3,2,1,0:T(8,128)(2,1)S(1)} collective-permute-done((bf16[4,1,128,256]{3,2,1,0:T(8,128)(2,1)S(1)}, bf16[4,1,128,256]{3,2,1,0:T(8,128)(2,1)S(1)}, u32[]{:S(2)}, u32[]{:S(2)}) %collective-permute-start) | collective-permute-done | bytes 262176 | tf_op jit(solution)/shard_map/ppermute | solution.py:34
  103.1 3.4 %collective-permute-done.1 = bf16[4,1,128,256]{3,2,1,0:T(8,128)(2,1)S(1)} collective-permute-done((bf16[4,1,128,256]{3,2,1,0:T(8,128)(2,1)S(1)}, bf16[4,1,128,256]{3,2,1,0:T(8,128)(2,1)S(1)}, u32[]{:S(2)}, u32[]{:S(2)}) %collective-permute-start.1) | collective-permute-done | bytes 262176 | tf_op jit(solution)/shard_map/ppermute | solution.py:35
  108.6 1.8 %fusion.3 = bf16[6,4,8,19,256]{4,1,3,2,0:T(4,128)(2,1)} fusion(bf16[6,4,7,2,256]{4,1,3,2,0:T(4,128)(2,1)S(1)} %slice.63, bf16[6,4,8,17,256]{4,1,3,2,0:T(4,128)(2,1)S(1)} %bitcast.155), kind=kLoop, calls=%fused_computation.10 | loop fusion | flops 5603328 | bytes 3710976 | tf_op jit(solution)/shard_map/conv_general_dilated | solution.py:58
  113.9 3.7 %all-to-all-start.1 = ((bf16[8,32,3,3,256,1]{4,1,3,2,5,0:T(8,128)(2,1)}), bf16[8,32,3,3,256,1]{4,1,3,2,5,0:T(8,128)(2,1)S(1)}, u32[]{:S(2)}, u32[]{:S(2)}) async-start(bf16[8,32,3,3,256,1]{4,1,3,2,5,0:T(8,128)(2,1)} %broadcast_in_dim.41), calls=%async_computation.1 | async-start | bytes 2359296 | tf_op jit(solution)/shard_map/all_to_all | solution.py:17
  118.9 2.0 %copy.206 = bf16[8,32,3,3,256,1]{4,0,1,3,2,5:T(8,128)(2,1)S(1)} copy(bf16[8,32,3,3,256,1]{4,1,3,2,5,0:T(8,128)(2,1)} %all-to-all-done.3) | data formatting | bytes 2359296 | tf_op jit(solution)/shard_map/all_to_all | solution.py:17
  120.9 1.6 copy.125
  122.4 2.4 %fusion.50 = (f32[2,32,9,256]{3,1,2,0:T(8,128)S(1)}, f32[2,32,9,256]{3,1,2,0:T(8,128)S(1)}) fusion(bf16[256,3,3,256,1]{0,3,2,1,4:T(8,128)(2,1)} %copy.125, bf16[4,4,8,11,256]{4,1,3,2,0:T(4,128)(2,1)} %fusion.18, pred[32,9]{0,1:T(8,128)(4,1)S(1)} %copy-done.16), kind=kOutput, calls=%fused_computation.86 | convolution fusion | flops 679772160 | bytes 3080480 | tf_op jit(solution)/shard_map/conv_general_dilated | solution.py:58
  126.4 6.4 %all-to-all-done.1 = bf16[8,32,3,3,256,1]{4,1,3,2,5,0:T(8,128)(2,1)S(1)} async-done(((bf16[8,32,3,3,256,1]{4,1,3,2,5,0:T(8,128)(2,1)}), bf16[8,32,3,3,256,1]{4,1,3,2,5,0:T(8,128)(2,1)S(1)}, u32[]{:S(2)}, u32[]{:S(2)}) %all-to-all-start.1) | async-done | bytes 1179680 | tf_op jit(solution)/shard_map/all_to_all | solution.py:17
  133.5 1.6 copy.118
  135.0 4.7 %fusion.49 = (f32[4,32,17,256]{3,1,2,0:T(8,128)S(1)}, f32[4,32,17,256]{3,1,2,0:T(8,128)S(1)}) fusion(bf16[256,3,3,256,1]{0,3,2,1,4:T(8,128)(2,1)} %copy.118, bf16[6,4,8,19,256]{4,1,3,2,0:T(4,128)(2,1)} %fusion.3, pred[32,17]{0,1:T(8,128)(4,1)S(1)} %copy-done.15), kind=kOutput, calls=%fused_computation.85 | convolution fusion | flops 2568028160 | bytes 7504416 | tf_op jit(solution)/shard_map/conv_general_dilated | solution.py:58
  139.8 1.4 copy.120
  141.7 1.4 copy.119
  144.6 12.5 %all_to_all.37 = f32[32,1,768]{2,1,0:T(1,128)S(1)} all-to-all(f32[32,1,768]{2,1,0:T(1,128)} %reshape.231), channel_id=1, replica_groups=mesh['dp'=8,'space_0'=4,'space_1'=4,'space_2'=2] {'space_0','space_1','s..., dimensions={0} | all-to-all | bytes 196608 | tf_op jit(solution)/shard_map/all_to_all | solution.py:17
  157.6 1.5 reduce.19
  166.1 1.4 copy.138
  168.0 1.7 copy.145
  (136 shorter events, 29.4 us)
Async XLA Ops:
  39.6 13.9 %all-to-all-start.2 = ((bf16[32,3,3,256,1]{3,2,1,4,0:T(4,128)(2,1)}), bf16[32,3,3,256,1]{3,2,1,4,0:T(4,128)(2,1)S(1)}, u32[]{:S(2)}, u32[]{:S(2)}) async-start(bf16[32,3,3,256,1]{3,2,1,4,0:T(4,128)(2,1)} %broadcast_in_dim.43), calls=%async_computation.2 | async-start | bytes 393216 | tf_op jit(solution)/shard_map/all_to_all | solution.py:17
  43.4 47.0 %collective-permute-start.4 = (bf16[4,1,32,256]{3,2,1,0:T(8,128)(2,1)}, bf16[4,1,32,256]{3,2,1,0:T(8,128)(2,1)}, u32[]{:S(2)}, u32[]{:S(2)}) collective-permute-start(bf16[4,1,32,256]{3,2,1,0:T(8,128)(2,1)} %param.14), channel_id=1, source_target_pairs={{0,1},{1,2},{2,3},{3,4},{4,5},{5,6},{6,7},{7,8},{8,9},{9,10},{10,1... | collective-permute-start | bytes 196616 | tf_op jit(solution)/shard_map/ppermute | solution.py:34
  49.7 42.7 %collective-permute-start.5 = (bf16[4,1,32,256]{3,2,1,0:T(8,128)(2,1)}, bf16[4,1,32,256]{3,2,1,0:T(8,128)(2,1)}, u32[]{:S(2)}, u32[]{:S(2)}) collective-permute-start(bf16[4,1,32,256]{3,2,1,0:T(8,128)(2,1)} %param.14), channel_id=1, source_target_pairs={{1,0},{2,1},{3,2},{4,3},{5,4},{6,5},{7,6},{8,7},{9,8},{10,9},{11,1... | collective-permute-start | bytes 196616 | tf_op jit(solution)/shard_map/ppermute | solution.py:35
  51.7 11.9 %copy-start.6 = (bf16[4,1,32,256]{3,2,1,0:T(8,128)(2,1)S(1)}, bf16[4,1,32,256]{3,2,1,0:T(8,128)(2,1)}, u32[]{:S(2)}) copy-start(bf16[4,1,32,256]{3,2,1,0:T(8,128)(2,1)} %param.14) | copy-start | bytes 196612
  53.4 1.2 copy-start.2
  54.6 9.2 %copy-start.5 = (bf16[4,2,64,256]{3,2,1,0:T(8,128)(2,1)S(1)}, bf16[4,2,64,256]{3,2,1,0:T(8,128)(2,1)}, u32[]{:S(2)}) copy-start(bf16[4,2,64,256]{3,2,1,0:T(8,128)(2,1)} %param.13) | copy-start | bytes 786436
  54.6 25.3 %all-to-all-start.5 = ((bf16[8,32,3,3,256,1]{4,1,3,2,5,0:T(8,128)(2,1)}), bf16[8,32,3,3,256,1]{4,1,3,2,5,0:T(8,128)(2,1)S(1)}, u32[]{:S(2)}, u32[]{:S(2)}) async-start(bf16[8,32,3,3,256,1]{4,1,3,2,5,0:T(8,128)(2,1)} %broadcast_in_dim.93), calls=%async_computation.5 | async-start | bytes 2359296 | tf_op jit(solution)/shard_map/all_to_all | solution.py:17
  64.6 29.9 %collective-permute-start.2 = (bf16[4,1,64,256]{3,2,1,0:T(8,128)(2,1)}, bf16[4,1,64,256]{3,2,1,0:T(8,128)(2,1)}, u32[]{:S(2)}, u32[]{:S(2)}) collective-permute-start(bf16[4,1,64,256]{3,2,1,0:T(8,128)(2,1)} %get-tuple-element.17), channel_id=1, source_target_pairs={{0,1},{1,2},{2,3},{3,4},{4,5},{5,6},{6,7},{7,8},{8,9},{9,10},{10,1... | collective-permute-start | bytes 393224 | tf_op jit(solution)/shard_map/ppermute | solution.py:34
  68.1 26.4 %collective-permute-start.3 = (bf16[4,1,64,256]{3,2,1,0:T(8,128)(2,1)}, bf16[4,1,64,256]{3,2,1,0:T(8,128)(2,1)}, u32[]{:S(2)}, u32[]{:S(2)}) collective-permute-start(bf16[4,1,64,256]{3,2,1,0:T(8,128)(2,1)} %get-tuple-element.18), channel_id=1, source_target_pairs={{1,0},{2,1},{3,2},{4,3},{5,4},{6,5},{7,6},{8,7},{9,8},{10,9},{11,1... | collective-permute-start | bytes 393224 | tf_op jit(solution)/shard_map/ppermute | solution.py:35
  73.3 2.2 %copy-start.3 = (bf16[32,3,3,256,1]{3,2,1,4,0:T(4,128)(2,1)S(1)}, bf16[32,3,3,256,1]{3,2,1,4,0:T(4,128)(2,1)}, u32[]{:S(2)}) copy-start(bf16[32,3,3,256,1]{3,2,1,4,0:T(4,128)(2,1)} %copy-done.2) | copy-start | bytes 442372
  81.1 11.3 %copy-start.7 = (bf16[4,1,32,256]{3,2,1,0:T(8,128)(2,1)S(1)}, bf16[4,1,32,256]{3,2,1,0:T(8,128)(2,1)}, u32[]{:S(2)}) copy-start(bf16[4,1,32,256]{3,2,1,0:T(8,128)(2,1)} %param.14) | copy-start | bytes 196612
  81.1 31.5 %all-to-all-start.3 = ((bf16[8,32,3,3,256,1]{4,1,3,2,5,0:T(8,128)(2,1)}), bf16[8,32,3,3,256,1]{4,1,3,2,5,0:T(8,128)(2,1)}, u32[]{:S(2)}, u32[]{:S(2)}) async-start(bf16[8,32,3,3,256,1]{4,1,3,2,5,0:T(8,128)(2,1)} %broadcast_in_dim.89), calls=%async_computation.3 | async-start | bytes 2359296 | tf_op jit(solution)/shard_map/all_to_all | solution.py:17
  86.9 16.2 %collective-permute-start = (bf16[4,1,128,256]{3,2,1,0:T(8,128)(2,1)S(1)}, bf16[4,1,128,256]{3,2,1,0:T(8,128)(2,1)S(1)}, u32[]{:S(2)}, u32[]{:S(2)}) collective-permute-start(bf16[4,1,128,256]{3,2,1,0:T(8,128)(2,1)S(1)} %get-tuple-element.15), channel_id=1, source_target_pairs={{0,1},{1,2},{2,3},{3,4},{4,5},{5,6},{6,7},{7,8},{8,9},{9,10},{10,1... | collective-permute-start | bytes 786440 | tf_op jit(solution)/shard_map/ppermute | solution.py:34
  90.5 16.0 %collective-permute-start.1 = (bf16[4,1,128,256]{3,2,1,0:T(8,128)(2,1)S(1)}, bf16[4,1,128,256]{3,2,1,0:T(8,128)(2,1)S(1)}, u32[]{:S(2)}, u32[]{:S(2)}) collective-permute-start(bf16[4,1,128,256]{3,2,1,0:T(8,128)(2,1)S(1)} %get-tuple-element.16), channel_id=1, source_target_pairs={{1,0},{2,1},{3,2},{4,3},{5,4},{6,5},{7,6},{8,7},{9,8},{10,9},{11,1... | collective-permute-start | bytes 786440 | tf_op jit(solution)/shard_map/ppermute | solution.py:35
  108.6 1.8 %copy-start.1 = (bf16[32,3,3,256,1]{3,2,1,4,0:T(4,128)(2,1)S(1)}, bf16[32,3,3,256,1]{3,2,1,4,0:T(4,128)(2,1)}, u32[]{:S(2)}) copy-start(bf16[32,3,3,256,1]{3,2,1,4,0:T(4,128)(2,1)} %all_to_all.35) | copy-start | bytes 442372
  111.8 0.9 copy-start.4
  112.5 5.1 %copy-start = (bf16[3,4,8,7,256]{4,1,3,2,0:T(4,128)(2,1)S(1)}, bf16[3,4,8,7,256]{4,1,3,2,0:T(4,128)(2,1)}, u32[]{:S(2)}) copy-start(bf16[3,4,8,7,256]{4,1,3,2,0:T(4,128)(2,1)} %fusion.24) | copy-start | bytes 1032196
  112.5 5.1 %copy-start.14 = (pred[32,5]{0,1:T(8,128)(4,1)S(1)}, pred[32,5]{0,1:T(8,128)(4,1)}, u32[]{:S(2)}) copy-start(pred[32,5]{0,1:T(8,128)(4,1)} %constant.37) | copy-start | bytes 484
  113.9 18.9 %all-to-all-start.1 = ((bf16[8,32,3,3,256,1]{4,1,3,2,5,0:T(8,128)(2,1)}), bf16[8,32,3,3,256,1]{4,1,3,2,5,0:T(8,128)(2,1)S(1)}, u32[]{:S(2)}, u32[]{:S(2)}) async-start(bf16[8,32,3,3,256,1]{4,1,3,2,5,0:T(8,128)(2,1)} %broadcast_in_dim.41), calls=%async_computation.1 | async-start | bytes 2359296 | tf_op jit(solution)/shard_map/all_to_all | solution.py:17
  118.8 3.6 %copy-start.16 = (pred[32,9]{0,1:T(8,128)(4,1)S(1)}, pred[32,9]{0,1:T(8,128)(4,1)}, u32[]{:S(2)}) copy-start(pred[32,9]{0,1:T(8,128)(4,1)} %constant.36) | copy-start | bytes 868
  126.3 8.7 %copy-start.15 = (pred[32,17]{0,1:T(8,128)(4,1)S(1)}, pred[32,17]{0,1:T(8,128)(4,1)}, u32[]{:S(2)}) copy-start(pred[32,17]{0,1:T(8,128)(4,1)} %constant.35) | copy-start | bytes 1636
  143.3 18.3 %copy-start.8 = (f32[256]{0:T(256)S(1)}, f32[256]{0:T(256)}, u32[]{:S(2)}) copy-start(f32[256]{0:T(256)} %param.23) | copy-start | bytes 3076
  143.4 18.3 %copy-start.9 = (f32[256]{0:T(256)S(1)}, f32[256]{0:T(256)}, u32[]{:S(2)}) copy-start(f32[256]{0:T(256)} %param.22) | copy-start | bytes 3076
  160.5 2.4 %copy-start.10 = (f32[256]{0:T(256)S(1)}, f32[256]{0:T(256)}, u32[]{:S(2)}) copy-start(f32[256]{0:T(256)} %param.21) | copy-start | bytes 3076
  160.5 2.4 %copy-start.11 = (f32[256]{0:T(256)S(1)}, f32[256]{0:T(256)}, u32[]{:S(2)}) copy-start(f32[256]{0:T(256)} %param.20) | copy-start | bytes 3076
  164.6 0.7 copy-start.12
  164.6 0.7 copy-start.13
where the time goes:
time: 171 us; the launch traced here: 170 us
  blocking collectives  48.5 us (28%)
  starting transfers between devices  41.4 us (24%)
  local copies, waits for them, and re-layouts  37.2 us (22%)
  waiting for transfers between devices  21.5 us (13%)
  other arithmetic  12.3 us (7%)
  matrix products  7.46 us (4%)
    all_to_all x3, blocking collectives, sent_to_all(): lax.all_to_all(jnp.broadcast_to(array[None], (devices, *array.shape)), ax...  48.5 us
    all_to_all x4, starting transfers between devices, sent_to_all(): lax.all_to_all(jnp.broadcast_to(array[None], (devices, *array.shape)), ax...  22.3 us
    ppermute x3, starting transfers between devices, extended(): before = lax.ppermute(last, axis, up)  13.3 us
    all_to_all x4, waiting for transfers between devices, sent_to_all(): lax.all_to_all(jnp.broadcast_to(array[None], (devices, *array.shape)), ax...  12.5 us
    conv_general_dilated x3, matrix products, convolve(): lax.conv_general_dilated(padded, kernel, (1, 1), (margin, (1, 1)), dimens...  7.46 us
    unnamed x47, local copies, waits for them, and re-layouts  7.35 us
    broadcast_in_dim x10, local copies, waits for them, and re-layouts, sent_to_all(): jnp.broadcast_to(array[None], (devices, *array.shape))  7.23 us
    ppermute x3, starting transfers between devices, extended(): after = lax.ppermute(first, axis, down)  5.77 us
  transfers between devices with their start and end apart: 10, of which 5 were waited for; matrix products, arithmetic and copies ran while one was open for 17% of the time, Pallas kernels for 0%

commit v1 on v0

v1 whole, which is shorter than its diff:
```python
import jax
import jax.numpy as jnp
from jax import lax
from jax.experimental import pallas as pl
from jax.experimental.pallas import tpu as pltpu
from jax.sharding import Mesh
from jax.sharding import PartitionSpec as P

SPACE = ("x", "y", "c")
AXES = ("z", "x", "y", "c")
MESH = pl.DeviceIdType.MESH
NZ, NX, NY, NC = 8, 4, 4, 2
STRIPS = NX * NY * NC
C, G, B = 256, 32, 4
HALF = 128
LEVELS = ((4, 128), (2, 64), (1, 32))
epsilon = 1e-05
F32, BF16 = jnp.float32, jnp.bfloat16


def wrap(value, size):
    return lax.rem(value + 2 * size, size)


def put(ref, image, row, value):
    n = value.shape[0]
    rounded = value.astype(BF16)
    wide = rounded.astype(F32)
    place = lax.broadcasted_iota(jnp.int32, wide.shape, 0)
    ref[1, image, row] = rounded
    ref[0, image, row] = jnp.where(place == 0, 0.0, pltpu.roll(wide, 1, 0)).astype(BF16)
    ref[2, image, row] = jnp.where(place == n - 1, 0.0, pltpu.roll(wide, n - 1, 0)).astype(BF16)


def repeat_matrix(n):
    rows = lax.broadcasted_iota(jnp.int32, (2 * n, n), 0)
    columns = lax.broadcasted_iota(jnp.int32, (2 * n, n), 1)
    return (lax.shift_right_logical(rows, 1) == columns).astype(F32).astype(BF16)


def kernel(
    lat3, lat4, lat5, w3, w4, w5,
    f3, f4, f5, center_ref, scale_ref,
    w_all, w_tap, raw, l3, l4, l5, h3, h4, h5, x3, x4, x5, sums, stat_a, stat_b,
    local_sem, raw_send, raw_recv, z_send, z_recv, x_send, x_recv, c_send, c_recv,
    halo_send, halo_recv, stat_send, stat_recv,
):
    z, x, y, c = (lax.axis_index(a) for a in AXES)
    slot = y * 2 + c
    other = 1 - c
    strip = (x * NY + y) * 2 + c
    nxt, prv = wrap(strip + 1, STRIPS), wrap(strip - 1, STRIPS)
    next_id = (z, nxt // 8, lax.rem(nxt // 2, 4), lax.rem(nxt, 2))
    prev_id = (z, prv // 8, lax.rem(prv // 2, 4), lax.rem(prv, 2))
    partner = (z, x, y, other)

    ring_ids = [(z, x, wrap(y + dy, NY), k) for dy in (1, 2, 3) for k in range(2)] + [partner]
    x_ids = [(z, wrap(x + d, NX), y, c) for d in (1, 2, 3)]
    z_ids = [(wrap(z + d, NZ), x, y, c) for d in range(1, NZ)]

    barrier = pltpu.get_barrier_semaphore()
    greeted = z_ids + x_ids + ring_ids + [next_id, prev_id]
    for who in greeted:
        pl.semaphore_signal(barrier, 1, device_id=who, device_id_type=MESH)

    loads = [
        pltpu.make_async_copy(lat5, l5, local_sem.at[0]),
        pltpu.make_async_copy(lat4, l4, local_sem.at[1]),
        pltpu.make_async_copy(lat3, l3, local_sem.at[2]),
    ]
    for copy in loads:
        copy.start()

    first = strip == 0
    last = strip == STRIPS - 1
    up5, up4 = repeat_matrix(32), repeat_matrix(64)

    def rows5(image, row, source, hidden=None):
        value = source.astype(F32)
        if hidden is not None:
            value = jnp.where(hidden, 0.0, value)
        put(x5, image, row, value)

    def rows4(image, row, source, coarse, hidden=None):
        value = source.astype(F32) + jnp.dot(up5, coarse, preferred_element_type=F32)
        if hidden is not None:
            value = jnp.where(hidden, 0.0, value)
        put(x4, image, row, value)

    def rows3(image, row, source, hidden=None):
        middle = x4[1, image, (row + 1) // 2]
        value = source.astype(F32) + jnp.dot(up4, middle, preferred_element_type=F32)
        if hidden is not None:
            value = jnp.where(hidden, 0.0, value)
        put(x3, image, row, value)

    loads[0].wait()
    loads[1].wait()

    def own_coarse(image, _):
        rows5(image, 1, l5[image, 0])
        for q in (1, 2):
            rows4(image, q, l4[image, q - 1], l5[image, 0])
        return 0

    lax.fori_loop(0, B, own_coarse, 0)

    pl.semaphore_wait(barrier, len(greeted))

    weights = (w3, w4, w5)
    raw_copies = []
    mine = pl.ds(pl.multiple_of(c * HALF, HALF), HALF)
    theirs = pl.ds(pl.multiple_of(other * HALF, HALF), HALF)
    for level in range(3):
        keep = pltpu.make_async_copy(
            weights[level].at[:, :, mine], raw.at[slot, level], local_sem.at[3 + level]
        )
        keep.start()
        raw_copies.append(keep)
    raw_remote = []
    for level in range(3):
        for dy in (1, 2, 3):
            for k in range(2):
                raw_remote.append(
                    pltpu.make_async_remote_copy(
                        weights[level].at[:, :, k * HALF : (k + 1) * HALF],
                        raw.at[slot, level],
                        raw_send.at[level, (dy - 1) * 2 + k],
                        raw_recv.at[level, (dy - 1) * 2 + c],
                        device_id=(z, x, wrap(y + dy, NY), k),
                        device_id_type=MESH,
                    )
                )
        raw_remote.append(
            pltpu.make_async_remote_copy(
                weights[level].at[:, :, theirs],
                raw.at[slot, level],
                raw_send.at[level, 6],
                raw_recv.at[level, 6],
                device_id=partner,
                device_id_type=MESH,
            )
        )
    for copy in raw_remote:
        copy.start()

    halo = []
    for number, (source, target, who) in enumerate((
        (lat5.at[:, 0], h5.at[0], next_id),
        (lat5.at[:, 0], h5.at[1], prev_id),
        (lat4.at[:, 1], h4.at[0], next_id),
        (lat4.at[:, 0], h4.at[1], prev_id),
        (lat3.at[:, 3], h3.at[0], next_id),
        (lat3.at[:, 0], h3.at[1], prev_id),
    )):
        copy = pltpu.make_async_remote_copy(
            source, target, halo_send.at[number], halo_recv.at[number],
            device_id=who, device_id_type=MESH,
        )
        copy.start()
        halo.append(copy)

    loads[2].wait()

    def own_fine(image, _):
        for r in (1, 2, 3, 4):
            rows3(image, r, l3[image, r - 1])
        return 0

    lax.fori_loop(0, B, own_fine, 0)

    z_copies, x_copies, c_copies = {}, {}, {}
    for level in range(3):
        raw_copies[level].wait()
        for i in range(7):
            pltpu.make_async_remote_copy(
                raw.at[0, level], raw.at[0, level],
                raw_send.at[level, i], raw_recv.at[level, i],
                device_id=partner, device_id_type=MESH,
            ).wait_recv()
        for kh in range(3):
            rows = [raw[s, level, kh].astype(F32) for s in range(8)]
            for kw in range(3):
                tile = jnp.concatenate([r[kw : kw + 1] for r in rows], axis=0)
                w_all[c, level, x, z, kh * 3 + kw] = tile.astype(BF16)
        for d in range(1, NZ):
            copy = pltpu.make_async_remote_copy(
                w_all.at[c, level, x, z], w_all.at[c, level, x, z],
                z_send.at[level, d - 1], z_recv.at[level, d - 1],
                device_id=z_ids[d - 1], device_id_type=MESH,
            )
            z_copies[level, d] = copy
    for level in range(3):
        for d in (4, 3, 5, 2, 6, 1, 7):
            z_copies[level, d].start()

    for copy in halo:
        copy.wait_recv()

    def outer(image, _):
        rows5(image, 0, h5[0, image], first)
        rows5(image, 2, h5[1, image], last)
        rows4(image, 0, h4[0, image], h5[0, image], first)
        rows4(image, 3, h4[1, image], h5[1, image], last)
        rows3(image, 0, h3[0, image], first)
        rows3(image, 5, h3[1, image], last)
        return 0

    lax.fori_loop(0, B, outer, 0)

    def piece_to_partner(level, d):
        where = wrap(x - d, NX)
        copy = pltpu.make_async_remote_copy(
            w_all.at[c, level, where], w_all.at[c, level, where],
            c_send.at[level, d], c_recv.at[level, d],
            device_id=partner, device_id_type=MESH,
        )
        copy.start()
        c_copies[level, d] = copy

    for level in range(3):
        for d in range(1, NZ):
            z_copies[level, d].wait_recv()
        for d in (2, 1, 3):
            copy = pltpu.make_async_remote_copy(
                w_all.at[c, level, x], w_all.at[c, level, x],
                x_send.at[level, d - 1], x_recv.at[level, d - 1],
                device_id=x_ids[d - 1], device_id_type=MESH,
            )
            copy.start()
            x_copies[level, d] = copy
        piece_to_partner(level, 0)

    def receive_x(level):
        for d in (1, 3, 2):
            x_copies[level, d].wait_recv()
            piece_to_partner(level, d)

    def receive_partner(level):
        for d in range(NX):
            c_copies[level, d].wait_recv()

    def ready(level):
        def tap(t, _):
            for half in range(2):
                for o in range(0, 32, 2):
                    pair = [
                        w_all[half, level, (o + k) % 4, (o + k) // 4, t].astype(F32) for k in range(2)
                    ]
                    w_tap[t, o * 8 : o * 8 + 16, half * HALF : (half + 1) * HALF] = jnp.concatenate(
                        pair, axis=0
                    ).astype(BF16)
            return 0

        lax.fori_loop(0, 9, tap, 0)

    def product(left, t):
        return lax.dot_general(
            left, w_tap[t], (((1,), (1,)), ((), ())), preferred_element_type=F32
        )

    def conv3(image, _):
        total = None
        for t in range(9):
            kh, kw = t // 3, t % 3
            left = x3[kw, image, kh : kh + 4].reshape(4 * 128, C)
            part = product(left, t)
            total = part if total is None else total + part
        f3[image] = total.reshape(4, 128, C)
        sums[0, pl.ds(image, 1)] = jnp.sum(total, axis=0, keepdims=True)
        sums[1, pl.ds(image, 1)] = jnp.sum(total * total, axis=0, keepdims=True)
        return 0

    def conv_small(level, source, target):
        rows, width = LEVELS[level]
        total = None
        for t in range(9):
            kh, kw = t // 3, t % 3
            left = source[kw, :, kh : kh + rows].reshape(B * rows * width, C)
            part = product(left, t)
            total = part if total is None else total + part
        target[...] = total.reshape(B, rows, width, C)
        for image in range(B):
            one = total[image * rows * width : (image + 1) * rows * width]
            sums[2 * level, image : image + 1] = jnp.sum(one, axis=0, keepdims=True)
            sums[2 * level + 1, image : image + 1] = jnp.sum(one * one, axis=0, keepdims=True)

    receive_x(0)
    receive_partner(0)
    ready(0)
    lax.fori_loop(0, 2, conv3, 0)
    receive_x(1)
    lax.fori_loop(2, B, conv3, 0)
    receive_partner(1)
    ready(1)
    conv_small(1, x4, f4)
    receive_x(2)
    receive_partner(2)
    ready(2)
    conv_small(2, x5, f5)

    channel = lax.broadcasted_iota(jnp.int32, (C, 128), 0)
    lane = lax.broadcasted_iota(jnp.int32, (C, 128), 1)
    member = lax.shift_right_logical(channel, 3)

    def selector(image):
        return (lane == member + 32 * image).astype(F32)

    packed = jnp.zeros((8, 128), F32)
    for image in range(B):
        packed += lax.dot_general(
            sums[:, image], selector(image), (((1,), (0,)), ((), ())),
            precision=lax.Precision.HIGHEST, preferred_element_type=F32,
        )
    stat_a[slot] = packed
    stats = []
    for i, (dy, k) in enumerate([(dy, k) for dy in (1, 2, 3) for k in range(2)] + [(0, None)]):
        copy = pltpu.make_async_remote_copy(
            stat_a.at[slot], stat_a.at[slot],
            stat_send.at[i], stat_recv.at[6 if k is None else (dy - 1) * 2 + c],
            device_id=ring_ids[i], device_id_type=MESH,
        )
        copy.start()
        stats.append(copy)
    for i in range(7):
        pltpu.make_async_remote_copy(
            stat_a.at[0], stat_a.at[0], stat_send.at[i], stat_recv.at[i],
            device_id=partner, device_id_type=MESH,
        ).wait_recv()
    stat_b[x] = jnp.sum(stat_a[...], axis=0)
    for d in (1, 2, 3):
        copy = pltpu.make_async_remote_copy(
            stat_b.at[x], stat_b.at[x], stat_send.at[6 + d], stat_recv.at[6 + d],
            device_id=x_ids[d - 1], device_id_type=MESH,
        )
        copy.start()
        stats.append(copy)
    for copy in stats[7:]:
        copy.wait_recv()
    whole = jnp.sum(stat_b[...], axis=0)

    spreads = []
    for level, (rows, width) in enumerate(LEVELS):
        volume = float(rows * STRIPS * width * (C // G))
        mean = whole[2 * level : 2 * level + 1] / volume
        square = whole[2 * level + 1 : 2 * level + 2] / volume
        spread = jnp.maximum(square - mean * mean, 0.0)
        spreads += [mean, lax.rsqrt(spread + epsilon)]
    spreads += [jnp.zeros((2, 128), F32)]
    table = jnp.concatenate(spreads, axis=0)
    for image in range(B):
        spread_out = lax.dot_general(
            table, selector(image), (((1,), (1,)), ((), ())),
            precision=lax.Precision.HIGHEST, preferred_element_type=F32,
        )
        for level in range(3):
            center_ref[level, image : image + 1] = spread_out[2 * level : 2 * level + 1]
            scale_ref[level, image : image + 1] = spread_out[2 * level + 1 : 2 * level + 2]

    for group in (raw_remote, halo, z_copies.values(), x_copies.values(), c_copies.values(), stats):
        for copy in group:
            copy.wait_send()


def local(
    lateral3, lateral4, lateral5, conv_weight3, conv_weight4, conv_weight5,
    norm_gain3, norm_shift3, norm_gain4, norm_shift4, norm_gain5, norm_shift5,
):
    dma = pltpu.SemaphoreType.DMA
    vmem = pl.BlockSpec(memory_space=pltpu.VMEM)
    anywhere = pl.BlockSpec(memory_space=pl.ANY)
    f3, f4, f5, center, scale = pl.pallas_call(
        kernel,
        out_shape=[jax.ShapeDtypeStruct((B, r, w, C), F32) for r, w in LEVELS]
        + [jax.ShapeDtypeStruct((3, B, C), F32)] * 2,
        in_specs=[anywhere] * 3 + [vmem] * 3,
        out_specs=[vmem] * 5,
        scratch_shapes=[
            pltpu.VMEM((2, 3, NX, NZ, 9, 8, HALF), BF16),
            pltpu.VMEM((9, C, C), BF16),
            pltpu.VMEM((8, 3, 3, 3, HALF), BF16),
            pltpu.VMEM((B, 4, 128, C), BF16),
            pltpu.VMEM((B, 2, 64, C), BF16),
            pltpu.VMEM((B, 1, 32, C), BF16),
            pltpu.VMEM((2, B, 128, C), BF16),
            pltpu.VMEM((2, B, 64, C), BF16),
            pltpu.VMEM((2, B, 32, C), BF16),
            pltpu.VMEM((3, B, 6, 128, C), BF16),
            pltpu.VMEM((3, B, 4, 64, C), BF16),
            pltpu.VMEM((3, B, 3, 32, C), BF16),
            pltpu.VMEM((8, B, C), F32),
            pltpu.VMEM((8, 8, 128), F32),
            pltpu.VMEM((NX, 8, 128), F32),
            dma((6,)),
            dma((3, 7)), dma((3, 7)),
            dma((3, 7)), dma((3, 7)),
            dma((3, 3)), dma((3, 3)),
            dma((3, 4)), dma((3, 4)),
            dma((6,)), dma((6,)),
            dma((10,)), dma((10,)),
        ],
        compiler_params=pltpu.CompilerParams(
            collective_id=0, has_side_effects=True, vmem_limit_bytes=48 * 2**20
        ),
        name="neck",
    )(
        lateral3, lateral4, lateral5,
        conv_weight3.reshape(3, 3, C), conv_weight4.reshape(3, 3, C), conv_weight5.reshape(3, 3, C),
    )

    def normalize(values, level, gain, shift):
        deviation = values - center[level][:, None, None, :]
        return deviation * scale[level][:, None, None, :] * gain + shift

    return (
        normalize(f3, 0, norm_gain3, norm_shift3),
        normalize(f4, 1, norm_gain4, norm_shift4),
        normalize(f5, 2, norm_gain5, norm_shift5),
    )


def solution(mesh):
    torus = Mesh(mesh.devices.reshape(NZ, NX, NY, NC), AXES)
    strips = P("z", SPACE, None, None)
    kernels = P(None, None, None, AXES)
    return jax.shard_map(
        local,
        mesh=torus,
        in_specs=(strips,) * 3 + (kernels,) * 3 + (P(),) * 6,
        out_specs=(strips,) * 3,
        check_vma=False,
    )
```

time: 171 us -> 65.5 us (0.38)
  Pallas kernels: 0 us -> 54.8 us
  blocking collectives: 48.5 us -> 0 us
  starting transfers between devices: 41.4 us -> 0 us
  local copies, waits for them, and re-layouts: 37.2 us -> 5.11 us
  waiting for transfers between devices: 21.5 us -> 0 us
  other arithmetic: 12.3 us -> 4.62 us
  matrix products: 7.46 us -> 0 us
    pallas_call x0 -> x1, Pallas kernels: none -> 54.8 us  [local(): pl.pallas_call(kernel, out_shape=[jax.ShapeDtypeStruct((B, r, w, C), F32)...]
    all_to_all x3 -> x0, blocking collectives: 48.5 us -> none  [sent_to_all(): lax.all_to_all(jnp.broadcast_to(array[None], (devices, *array.shape)), ax...]
    all_to_all x4 -> x0, starting transfers between devices: 22.3 us -> none  [sent_to_all(): lax.all_to_all(jnp.broadcast_to(array[None], (devices, *array.shape)), ax...]
    ppermute x6 -> x0, starting transfers between devices: 19.1 us -> none  [the longest x3 13.3 us: extended(): before = lax.ppermute(last, axis, up)]
    all_to_all x4 -> x0, waiting for transfers between devices: 12.5 us -> none  [sent_to_all(): lax.all_to_all(jnp.broadcast_to(array[None], (devices, *array.shape)), ax...]
    ppermute x6 -> x0, waiting for transfers between devices: 9.06 us -> none  [the longest x3 5.68 us: extended(): before = lax.ppermute(last, axis, up)]
    broadcast_in_dim x13 -> x0, local copies, waits for them, and re-layouts: 8.15 us -> none  [the longest x10 7.23 us: sent_to_all(): jnp.broadcast_to(array[None], (devices, *array.shape))]
    conv_general_dilated x3 -> x0, matrix products: 7.46 us -> none  [convolve(): lax.conv_general_dilated(padded, kernel, (1, 1), (margin, (1, 1)), dimens...]
  transfers between devices with their start and end apart: 10 -> 0, of which waited for: 5 -> 0; matrix products, arithmetic and copies ran while one was open for 17% -> 0% of each run, Pallas kernels for 0% -> 0%
where the time goes in v1:
time: 65.5 us; the launch traced here: 65.2 us
  Pallas kernels  54.8 us (84%)
  local copies, waits for them, and re-layouts  5.11 us (8%)
  other arithmetic  4.62 us (7%)
  between operations  0.68 us (1%)
    pallas_call x1, Pallas kernels, local(): pl.pallas_call(kernel, out_shape=[jax.ShapeDtypeStruct((B, r, w, C), F32)...  54.8 us
    unnamed x16, local copies, waits for them, and re-layouts  5.1 us
    add x3, other arithmetic, normalize(): return deviation * scale[level][:, None, None, :] * gain + shift  4.62 us

profile of v1, /device:TPU:1, one launch (start us, length us, event | category | flops | bytes accessed | tf_op | source)
XLA Modules:
  0.0 65.2 jit_solution(8459837405029713752)
XLA Ops:
  0.6 0.0 copy-start.7
  0.6 0.0 copy-start.6
  0.7 0.0 copy-start
  0.7 1.2 %copy-done = bf16[4,4,128,256]{3,2,1,0:T(8,128)(2,1)S(1)} copy-done((bf16[4,4,128,256]{3,2,1,0:T(8,128)(2,1)S(1)}, bf16[4,4,128,256]{3,2,1,0:T(8,128)(2,1)}, u32[]{:S(2)}) %copy-start) | copy-done | bytes 1048600
  1.9 0.0 copy-start.1
  1.9 0.9 %copy-done.1 = bf16[4,2,64,256]{3,2,1,0:T(8,128)(2,1)S(1)} copy-done((bf16[4,2,64,256]{3,2,1,0:T(8,128)(2,1)S(1)}, bf16[4,2,64,256]{3,2,1,0:T(8,128)(2,1)}, u32[]{:S(2)}) %copy-start.1) | copy-done | bytes 262168
  2.8 0.0 copy-start.2
  2.8 0.8 %copy-done.2 = bf16[4,1,32,256]{3,2,1,0:T(8,128)(2,1)S(1)} copy-done((bf16[4,1,32,256]{3,2,1,0:T(8,128)(2,1)S(1)}, bf16[4,1,32,256]{3,2,1,0:T(8,128)(2,1)}, u32[]{:S(2)}) %copy-start.2) | copy-done | bytes 65560
  3.7 0.0 copy-start.3
  3.7 0.7 %copy-done.3 = bf16[3,3,256,1]{2,1,3,0:T(4,128)(2,1)S(1)} copy-done((bf16[3,3,256,1]{2,1,3,0:T(4,128)(2,1)S(1)}, bf16[3,3,256,1]{2,1,3,0:T(4,128)(2,1)}, u32[]{:S(2)}) %copy-start.3) | copy-done | bytes 4632
  4.4 0.0 copy-start.4
  4.4 0.7 %copy-done.4 = bf16[3,3,256,1]{2,1,3,0:T(4,128)(2,1)S(1)} copy-done((bf16[3,3,256,1]{2,1,3,0:T(4,128)(2,1)S(1)}, bf16[3,3,256,1]{2,1,3,0:T(4,128)(2,1)}, u32[]{:S(2)}) %copy-start.4) | copy-done | bytes 4632
  5.1 0.0 copy-start.5
  5.1 0.7 %copy-done.5 = bf16[3,3,256,1]{2,1,3,0:T(4,128)(2,1)S(1)} copy-done((bf16[3,3,256,1]{2,1,3,0:T(4,128)(2,1)S(1)}, bf16[3,3,256,1]{2,1,3,0:T(4,128)(2,1)}, u32[]{:S(2)}) %copy-start.5) | copy-done | bytes 4632
  5.8 54.8 %neck.1 = (f32[4,4,128,256]{3,2,1,0:T(8,128)S(1)}, f32[4,2,64,256]{3,2,1,0:T(8,128)S(1)}, f32[4,1,32,256]{3,2,1,0:T(8,128)S(1)}, f32[3,4,256]{2,1,0:T(4,128)S(1)}, f32[3,4,256]{2,1,0:T(4,128)S(1)}) custom-call(bf16[4,4,128,256]{3,2,1,0:T(8,128)(2,1)S(1)} %copy-done, bf16[4,2,64,256]{3,2,1,0:T(8,128)(2,1)S(1)} %copy-done.1, ...), custom_call_target="tpu_custom_call" | custom-call | tf_op jit(solution)/shard_map/neck/pallas_call | solution.py:372
  60.6 1.4 %multiply_add_fusion.2 = f32[4,1,32,256]{3,2,1,0:T(8,128)} fusion(f32[4,1,32,256]{3,2,1,0:T(8,128)S(1)} %get-tuple-element.12, f32[256]{0:T(256)} %param.23, f32[256]{0:T(256)} %param.22, f32[4,256]{1,0:T(4,128)S(1)} %get-tuple-element.16, f32[4,256]{1,0:T(4,128)S(1)} %get-tuple-element.21), kind=kLoop, calls=%fused_computation.2 | loop fusion | flops 131072 | bytes 272384 | tf_op jit(solution)/shard_map/add | solution.py:413
  61.9 1.6 %multiply_add_fusion.1 = f32[4,2,64,256]{3,2,1,0:T(8,128)} fusion(f32[4,2,64,256]{3,2,1,0:T(8,128)S(1)} %get-tuple-element.11, f32[256]{0:T(256)} %param.21, f32[256]{0:T(256)} %param.20, f32[4,256]{1,0:T(4,128)S(1)} %get-tuple-element.17, f32[4,256]{1,0:T(4,128)S(1)} %get-tuple-element.20), kind=kLoop, calls=%fused_computation.1 | loop fusion | flops 524288 | bytes 1058816 | tf_op jit(solution)/shard_map/add | solution.py:413
  63.5 0.0 copy-done.7
  63.5 0.0 copy-done.6
  63.5 1.7 %multiply_add_fusion = f32[4,4,128,256]{3,2,1,0:T(8,128)} fusion(f32[4,4,128,256]{3,2,1,0:T(8,128)S(1)} %get-tuple-element.8, f32[256]{0:T(256)S(1)} %copy-done.6, f32[256]{0:T(256)S(1)} %copy-done.7, f32[4,256]{1,0:T(4,128)S(1)} %get-tuple-element.18, f32[4,256]{1,0:T(4,128)S(1)} %get-tuple-element.19), kind=kLoop, calls=%fused_computation | loop fusion | flops 2097152 | bytes 4204544 | tf_op jit(solution)/shard_map/add | solution.py:413
  (1 shorter events, 0.0 us)
Async XLA Ops:
  0.6 62.9 %copy-start.7 = (f32[256]{0:T(256)S(1)}, f32[256]{0:T(256)}, u32[]{:S(2)}) copy-start(f32[256]{0:T(256)} %param.18) | copy-start | bytes 3076
  0.6 62.9 %copy-start.6 = (f32[256]{0:T(256)S(1)}, f32[256]{0:T(256)}, u32[]{:S(2)}) copy-start(f32[256]{0:T(256)} %param.19) | copy-start | bytes 3076
  0.7 1.2 %copy-start = (bf16[4,4,128,256]{3,2,1,0:T(8,128)(2,1)S(1)}, bf16[4,4,128,256]{3,2,1,0:T(8,128)(2,1)}, u32[]{:S(2)}) copy-start(bf16[4,4,128,256]{3,2,1,0:T(8,128)(2,1)} %lat3.1) | copy-start | bytes 3145732
  1.9 0.9 %copy-start.1 = (bf16[4,2,64,256]{3,2,1,0:T(8,128)(2,1)S(1)}, bf16[4,2,64,256]{3,2,1,0:T(8,128)(2,1)}, u32[]{:S(2)}) copy-start(bf16[4,2,64,256]{3,2,1,0:T(8,128)(2,1)} %lat4.1) | copy-start | bytes 786436
  2.8 0.8 %copy-start.2 = (bf16[4,1,32,256]{3,2,1,0:T(8,128)(2,1)S(1)}, bf16[4,1,32,256]{3,2,1,0:T(8,128)(2,1)}, u32[]{:S(2)}) copy-start(bf16[4,1,32,256]{3,2,1,0:T(8,128)(2,1)} %lat5.1) | copy-start | bytes 196612
  3.7 0.7 %copy-start.3 = (bf16[3,3,256,1]{2,1,3,0:T(4,128)(2,1)S(1)}, bf16[3,3,256,1]{2,1,3,0:T(4,128)(2,1)}, u32[]{:S(2)}) copy-start(bf16[3,3,256,1]{2,1,3,0:T(4,128)(2,1)} %param.15) | copy-start | bytes 13828
  4.4 0.7 %copy-start.4 = (bf16[3,3,256,1]{2,1,3,0:T(4,128)(2,1)S(1)}, bf16[3,3,256,1]{2,1,3,0:T(4,128)(2,1)}, u32[]{:S(2)}) copy-start(bf16[3,3,256,1]{2,1,3,0:T(4,128)(2,1)} %param.16) | copy-start | bytes 13828
  5.1 0.7 %copy-start.5 = (bf16[3,3,256,1]{2,1,3,0:T(4,128)(2,1)S(1)}, bf16[3,3,256,1]{2,1,3,0:T(4,128)(2,1)}, u32[]{:S(2)}) copy-start(bf16[3,3,256,1]{2,1,3,0:T(4,128)(2,1)} %param.17) | copy-start | bytes 13828

commit v2 on v1

v2 whole, which is shorter than its diff:
```python
import jax
import jax.numpy as jnp
from jax import lax
from jax.experimental import pallas as pl
from jax.experimental.pallas import tpu as pltpu
from jax.sharding import Mesh
from jax.sharding import PartitionSpec as P

SPACE = ("x", "y", "c")
AXES = ("z", "x", "y", "c")
MESH = pl.DeviceIdType.MESH
NZ, NX, NY, NC = 8, 4, 4, 2
STRIPS = NX * NY * NC
C, G, B = 256, 32, 4
HALF = 128
LEVELS = ((4, 128), (2, 64), (1, 32))
epsilon = 1e-05
F32, BF16 = jnp.float32, jnp.bfloat16


def wrap(value, size):
    return lax.rem(value + 2 * size, size)


def put(ref, image, row, value):
    n = value.shape[0]
    rounded = value.astype(BF16)
    wide = rounded.astype(F32)
    place = lax.broadcasted_iota(jnp.int32, wide.shape, 0)
    ref[1, image, row] = rounded
    ref[0, image, row] = jnp.where(place == 0, 0.0, pltpu.roll(wide, 1, 0)).astype(BF16)
    ref[2, image, row] = jnp.where(place == n - 1, 0.0, pltpu.roll(wide, n - 1, 0)).astype(BF16)


def repeat_matrix(n):
    rows = lax.broadcasted_iota(jnp.int32, (2 * n, n), 0)
    columns = lax.broadcasted_iota(jnp.int32, (2 * n, n), 1)
    return (lax.shift_right_logical(rows, 1) == columns).astype(F32).astype(BF16)


def kernel(
    lat3, lat4, lat5, w3, w4, w5, g3, b3, g4, b4, g5, b5,
    f3, f4, f5, table_ref,
    w_all, w_tap, raw, l3, l4, l5, h3, h4, h5, x3, x4, x5, sums, stat_a, stat_b, params,
    local_sem, raw_send, raw_recv, z_send, z_recv, x_send, x_recv, y_send, y_recv, c_send, c_recv,
    halo_send, halo_recv, stat_send, stat_recv,
):
    z, x, y, c = (lax.axis_index(a) for a in AXES)
    slot = y * 2 + c
    other = 1 - c
    strip = (x * NY + y) * 2 + c
    nxt, prv = wrap(strip + 1, STRIPS), wrap(strip - 1, STRIPS)
    next_id = (z, nxt // 8, lax.rem(nxt // 2, 4), lax.rem(nxt, 2))
    prev_id = (z, prv // 8, lax.rem(prv // 2, 4), lax.rem(prv, 2))
    partner = (z, x, y, other)

    ring_ids = [(z, x, wrap(y + dy, NY), k) for dy in (1, 2, 3) for k in range(2)] + [partner]
    y_ids = [(z, x, wrap(y + d, NY), c) for d in (1, 2, 3)]
    x_ids = [(z, wrap(x + d, NX), y, c) for d in (1, 2, 3)]
    z_ids = [(wrap(z + d, NZ), x, y, c) for d in range(1, NZ)]

    barrier = pltpu.get_barrier_semaphore()
    greeted = z_ids + x_ids + ring_ids + [next_id, prev_id]
    for who in greeted:
        pl.semaphore_signal(barrier, 1, device_id=who, device_id_type=MESH)

    loads = [
        pltpu.make_async_copy(lat5, l5, local_sem.at[0]),
        pltpu.make_async_copy(lat4, l4, local_sem.at[1]),
        pltpu.make_async_copy(lat3, l3, local_sem.at[2]),
    ]
    for copy in loads:
        copy.start()
    weights = (w3, w4, w5)
    mine = pl.ds(pl.multiple_of(c * HALF, HALF), HALF)
    theirs = pl.ds(pl.multiple_of(other * HALF, HALF), HALF)
    for level in range(3):
        pltpu.make_async_copy(
            weights[level].at[:, :, mine], raw.at[slot, level], local_sem.at[3]
        ).start()
    for i, source in enumerate((g3, b3, g4, b4, g5, b5)):
        pltpu.make_async_copy(source, params.at[i], local_sem.at[4]).start()

    def remote(source, target, sends, recvs, who):
        pltpu.make_async_remote_copy(
            source, target, sends, recvs, device_id=who, device_id_type=MESH
        ).start()

    def all_of(total, sends, recvs):
        return pltpu.make_async_remote_copy(
            total, total, sends, recvs, device_id=partner, device_id_type=MESH
        )

    with jax.named_scope("s3_barrier"):
        pl.semaphore_wait(barrier, len(greeted))

    for level in range(3):
        for dy in (2, 1, 3):
            for k in range(2):
                remote(
                    weights[level].at[:, :, k * HALF : (k + 1) * HALF], raw.at[slot, level],
                    raw_send.at[0], raw_recv.at[level], (z, x, wrap(y + dy, NY), k),
                )
        remote(
            weights[level].at[:, :, theirs], raw.at[slot, level],
            raw_send.at[0], raw_recv.at[level], partner,
        )

    for level, lateral, held, lowest in ((2, lat5, h5, 0), (1, lat4, h4, 1), (0, lat3, h3, 3)):
        remote(lateral.at[:, lowest], held.at[0], halo_send.at[level], halo_recv.at[level], next_id)
        remote(lateral.at[:, 0], held.at[1], halo_send.at[level], halo_recv.at[level], prev_id)

    first = strip == 0
    last = strip == STRIPS - 1
    up5, up4 = repeat_matrix(32), repeat_matrix(64)

    def rows5(image, row, source, hidden=None):
        value = source.astype(F32)
        if hidden is not None:
            value = jnp.where(hidden, 0.0, value)
        put(x5, image, row, value)

    def rows4(image, row, source, coarse, hidden=None):
        value = source.astype(F32) + jnp.dot(up5, coarse, preferred_element_type=F32)
        if hidden is not None:
            value = jnp.where(hidden, 0.0, value)
        put(x4, image, row, value)

    def rows3(image, row, source, hidden=None):
        middle = x4[1, image, (row + 1) // 2]
        value = source.astype(F32) + jnp.dot(up4, middle, preferred_element_type=F32)
        if hidden is not None:
            value = jnp.where(hidden, 0.0, value)
        put(x3, image, row, value)

    for copy in loads:
        copy.wait()

    def own(image, _):
        rows5(image, 1, l5[image, 0])
        for q in (1, 2):
            rows4(image, q, l4[image, q - 1], l5[image, 0])
        for r in (1, 2, 3, 4):
            rows3(image, r, l3[image, r - 1])
        return 0

    with jax.named_scope("s5_own"):
        lax.fori_loop(0, B, own, 0)

    DIRECT, SPLIT = slice(0, 4), slice(4, 9)
    quarter = pl.ds(2 * y, 2)
    pltpu.make_async_copy(raw.at[0], raw.at[0], local_sem.at[3]).wait()

    for level in range(3):
        with jax.named_scope(f"s6_raw{level}"):
            all_of(raw.at[0:7, level], raw_send.at[0], raw_recv.at[level]).wait_recv()
        for kh in range(3):
            rows = [raw[s, level, kh].astype(F32) for s in range(8)]
            for kw in range(3):
                tile = jnp.concatenate([r[kw : kw + 1] for r in rows], axis=0)
                w_all[c, level, x, z, kh * 3 + kw] = tile.astype(BF16)
        for part, taps in ((1, SPLIT), (0, DIRECT)):
            for d in (4, 3, 5, 2, 6, 1, 7):
                ref = w_all.at[c, level, x, z, taps]
                remote(ref, ref, z_send.at[0], z_recv.at[level, part], z_ids[d - 1])

    def outer(image, _):
        rows5(image, 0, h5[0, image], first)
        rows5(image, 2, h5[1, image], last)
        rows4(image, 0, h4[0, image], h5[0, image], first)
        rows4(image, 3, h4[1, image], h5[1, image], last)
        rows3(image, 0, h3[0, image], first)
        rows3(image, 5, h3[1, image], last)
        return 0

    def to_partner(level, part, ref):
        remote(ref, ref, c_send.at[0], c_recv.at[level, part], partner)

    def after_z(level, part):
        taps = SPLIT if part else DIRECT
        with jax.named_scope(f"z{level}{part}"):
            all_of(w_all.at[c, level, x, 0:7, taps], z_send.at[0], z_recv.at[level, part]).wait_recv()
        ref = w_all.at[c, level, x, quarter, taps] if part else w_all.at[c, level, x, :, taps]
        for d in (2, 1, 3):
            remote(ref, ref, x_send.at[part], x_recv.at[level, part], x_ids[d - 1])
        to_partner(level, part, w_all.at[c, level, x, :, taps])

    def after_x(level, part):
        with jax.named_scope(f"x{level}{part}"):
            if part:
                total = w_all.at[c, level, 0:3, 0:2, SPLIT]
            else:
                total = w_all.at[c, level, 0:3, :, DIRECT]
            all_of(total, x_send.at[part], x_recv.at[level, part]).wait_recv()
        for d in (1, 3, 2):
            where = wrap(x - d, NX)
            if part:
                ref = w_all.at[c, level, where, quarter, SPLIT]
                for e in (2, 1, 3):
                    remote(ref, ref, y_send.at[0], y_recv.at[level], y_ids[e - 1])
            else:
                to_partner(level, part, w_all.at[c, level, where, :, DIRECT])

    def after_y(level):
        with jax.named_scope(f"y{level}"):
            all_of(w_all.at[c, level, 0:3, 0:6, SPLIT], y_send.at[0], y_recv.at[level]).wait_recv()
        for d in (1, 2, 3):
            to_partner(level, 1, w_all.at[c, level, wrap(x - d, NX), :, SPLIT])

    def receive_partner(level, part):
        taps = SPLIT if part else DIRECT
        with jax.named_scope(f"c{level}{part}"):
            all_of(w_all.at[other, level, :, :, taps], c_send.at[0], c_recv.at[level, part]).wait_recv()

    def ready(level, part):
        def tap(t, _):
            for half in range(2):
                for o in range(0, 32, 2):
                    pair = [
                        w_all[half, level, (o + k) % 4, (o + k) // 4, t].astype(F32) for k in range(2)
                    ]
                    w_tap[t, o * 8 : o * 8 + 16, half * HALF : (half + 1) * HALF] = jnp.concatenate(
                        pair, axis=0
                    ).astype(BF16)
            return 0

        lax.fori_loop(4 * part, 9 if part else 4, tap, 0)

    def products(pick, part, start):
        total = start
        for t in range(9)[SPLIT if part else DIRECT]:
            term = lax.dot_general(
                pick(t // 3, t % 3), w_tap[t], (((1,), (1,)), ((), ())), preferred_element_type=F32
            )
            total = term if total is None else total + term
        return total

    def conv3(part):
        def step(image, _):
            total = products(
                lambda kh, kw: x3[kw, image, kh : kh + 4].reshape(4 * 128, C),
                part,
                f3[image].reshape(4 * 128, C) if part else None,
            )
            f3[image] = total.reshape(4, 128, C)
            if part:
                sums[0, pl.ds(image, 1)] = jnp.sum(total, axis=0, keepdims=True)
                sums[1, pl.ds(image, 1)] = jnp.sum(total * total, axis=0, keepdims=True)
            return 0

        return step

    def conv_small(level, part, source, target):
        rows, width = LEVELS[level]
        ready(level, part)
        total = products(
            lambda kh, kw: source[kw, :, kh : kh + rows].reshape(B * rows * width, C),
            part,
            target[...].reshape(B * rows * width, C) if part else None,
        )
        target[...] = total.reshape(B, rows, width, C)
        for image in range(B if part else 0):
            one = total[image * rows * width : (image + 1) * rows * width]
            sums[2 * level, image : image + 1] = jnp.sum(one, axis=0, keepdims=True)
            sums[2 * level + 1, image : image + 1] = jnp.sum(one * one, axis=0, keepdims=True)

    after_z(0, 1)
    with jax.named_scope("s7_halo"):
        for level, held in ((2, h5), (1, h4), (0, h3)):
            all_of(held, halo_send.at[level], halo_recv.at[level]).wait_recv()
    lax.fori_loop(0, 1, outer, 0)
    after_z(0, 0)
    lax.fori_loop(1, 2, outer, 0)
    after_z(1, 1)
    lax.fori_loop(2, B, outer, 0)
    after_x(0, 1)
    after_z(1, 0)
    after_x(0, 0)
    after_z(2, 1)
    after_x(1, 1)
    after_z(2, 0)
    receive_partner(0, 0)
    with jax.named_scope("conv3Aa"):
        ready(0, 0)
        lax.fori_loop(0, 2, conv3(0), 0)
    after_x(1, 0)
    with jax.named_scope("conv3Ab"):
        lax.fori_loop(2, B, conv3(0), 0)
    after_y(0)
    after_x(2, 1)
    receive_partner(0, 1)
    with jax.named_scope("conv3Ca"):
        ready(0, 1)
        lax.fori_loop(0, 2, conv3(1), 0)
    after_x(2, 0)
    after_y(1)
    with jax.named_scope("conv3Cb"):
        lax.fori_loop(2, B, conv3(1), 0)
    receive_partner(1, 0)
    with jax.named_scope("conv4A"):
        conv_small(1, 0, x4, f4)
    after_y(2)
    receive_partner(1, 1)
    with jax.named_scope("conv4C"):
        conv_small(1, 1, x4, f4)
    receive_partner(2, 0)
    receive_partner(2, 1)
    with jax.named_scope("conv5"):
        conv_small(2, 0, x5, f5)
        conv_small(2, 1, x5, f5)

    channel = lax.broadcasted_iota(jnp.int32, (C, 128), 0)
    lane = lax.broadcasted_iota(jnp.int32, (C, 128), 1)
    member = lax.shift_right_logical(channel, 3)

    def selector(image):
        return (lane == member + 32 * image).astype(F32)

    packed = jnp.zeros((8, 128), F32)
    for image in range(B):
        packed += lax.dot_general(
            sums[:, image], selector(image), (((1,), (0,)), ((), ())),
            precision=lax.Precision.HIGHEST, preferred_element_type=F32,
        )
    stat_a[slot] = packed
    for who in ring_ids:
        remote(stat_a.at[slot], stat_a.at[slot], stat_send.at[0], stat_recv.at[0], who)
    with jax.named_scope("u1_stat"):
        all_of(stat_a.at[0:7], stat_send.at[0], stat_recv.at[0]).wait_recv()
    stat_b[x] = jnp.sum(stat_a[...], axis=0)
    for who in x_ids:
        remote(stat_b.at[x], stat_b.at[x], stat_send.at[1], stat_recv.at[1], who)
    with jax.named_scope("u2_stat"):
        all_of(stat_b.at[0:3], stat_send.at[1], stat_recv.at[1]).wait_recv()
    whole = jnp.sum(stat_b[...], axis=0)

    with jax.named_scope("v1_table"):
        pltpu.make_async_copy(params, params, local_sem.at[4]).wait()
        spreads = []
        for level, (rows, width) in enumerate(LEVELS):
            volume = float(rows * STRIPS * width * (C // G))
            mean = whole[2 * level : 2 * level + 1] / volume
            square = whole[2 * level + 1 : 2 * level + 2] / volume
            spread = jnp.maximum(square - mean * mean, 0.0)
            spreads += [mean, lax.rsqrt(spread + epsilon)]
        spreads += [jnp.zeros((2, 128), F32)]
        table = jnp.concatenate(spreads, axis=0)
        for image in range(B):
            spread_out = lax.dot_general(
                table, selector(image), (((1,), (1,)), ((), ())),
                precision=lax.Precision.HIGHEST, preferred_element_type=F32,
            )
            for level in range(3):
                table_ref[level, 0, image : image + 1] = spread_out[2 * level : 2 * level + 1]
                table_ref[level, 1, image : image + 1] = (
                    spread_out[2 * level + 1 : 2 * level + 2] * params[2 * level]
                )
                table_ref[level, 2, image : image + 1] = params[2 * level + 1]

    with jax.named_scope("v2_sends"):
        all_of(raw.at[0:7], raw_send.at[0], raw_recv.at[0]).wait_send()
        for level, held in ((2, h5), (1, h4), (0, h3)):
            all_of(held, halo_send.at[level], halo_recv.at[level]).wait_send()
        all_of(w_all.at[c, :, 0, 0:7], z_send.at[0], z_recv.at[0, 0]).wait_send()
        all_of(w_all.at[c, :, 0:3, :, DIRECT], x_send.at[0], x_recv.at[0, 0]).wait_send()
        all_of(w_all.at[c, :, 0:3, 0:2, SPLIT], x_send.at[1], x_recv.at[0, 1]).wait_send()
        all_of(w_all.at[c, :, 0:3, 0:6, SPLIT], y_send.at[0], y_recv.at[0]).wait_send()
        all_of(w_all.at[c], c_send.at[0], c_recv.at[0, 0]).wait_send()
        all_of(stat_a.at[0:7], stat_send.at[0], stat_recv.at[0]).wait_send()
        all_of(stat_b.at[0:3], stat_send.at[1], stat_recv.at[1]).wait_send()


def finish(f3, f4, f5, table, o3, o4, o5, s3, s4, s5, sem):
    copies = []
    for level, (source, held, target) in enumerate(((f3, s3, o3), (f4, s4, o4), (f5, s5, o5))):
        for image in range(B):
            center = table[level, 0, image : image + 1][None]
            scale = table[level, 1, image : image + 1][None]
            shift = table[level, 2, image : image + 1][None]
            held[image] = (source[image] - center) * scale + shift
            copy = pltpu.make_async_copy(held.at[image], target.at[image], sem.at[level, image])
            copy.start()
            copies.append(copy)
    for copy in copies:
        copy.wait()


def local(
    lateral3, lateral4, lateral5, conv_weight3, conv_weight4, conv_weight5,
    norm_gain3, norm_shift3, norm_gain4, norm_shift4, norm_gain5, norm_shift5,
):
    dma = pltpu.SemaphoreType.DMA
    vmem = pl.BlockSpec(memory_space=pltpu.VMEM)
    hbm = pl.BlockSpec(memory_space=pltpu.HBM)
    shapes = [jax.ShapeDtypeStruct((B, r, w, C), F32) for r, w in LEVELS]
    operands = [lateral3, lateral4, lateral5]
    operands += [w.reshape(3, 3, C) for w in (conv_weight3, conv_weight4, conv_weight5)]
    operands += [
        v.reshape(1, C)
        for v in (norm_gain3, norm_shift3, norm_gain4, norm_shift4, norm_gain5, norm_shift5)
    ]
    filtered = pl.pallas_call(
        kernel,
        out_shape=shapes + [jax.ShapeDtypeStruct((3, 3, B, C), F32)],
        in_specs=[hbm] * 12,
        out_specs=[vmem] * 4,
        scratch_shapes=[
            pltpu.VMEM((2, 3, NX, NZ, 9, 8, HALF), BF16),
            pltpu.VMEM((9, C, C), BF16),
            pltpu.VMEM((8, 3, 3, 3, HALF), BF16),
            pltpu.VMEM((B, 4, 128, C), BF16),
            pltpu.VMEM((B, 2, 64, C), BF16),
            pltpu.VMEM((B, 1, 32, C), BF16),
            pltpu.VMEM((2, B, 128, C), BF16),
            pltpu.VMEM((2, B, 64, C), BF16),
            pltpu.VMEM((2, B, 32, C), BF16),
            pltpu.VMEM((3, B, 6, 128, C), BF16),
            pltpu.VMEM((3, B, 4, 64, C), BF16),
            pltpu.VMEM((3, B, 3, 32, C), BF16),
            pltpu.VMEM((8, B, C), F32),
            pltpu.VMEM((8, 8, 128), F32),
            pltpu.VMEM((NX, 8, 128), F32),
            pltpu.VMEM((6, 1, C), F32),
            dma((5,)),
            dma((1,)), dma((3,)),
            dma((1,)), dma((3, 2)),
            dma((2,)), dma((3, 2)),
            dma((1,)), dma((3,)),
            dma((1,)), dma((3, 2)),
            dma((3,)), dma((3,)),
            dma((2,)), dma((2,)),
        ],
        compiler_params=pltpu.CompilerParams(
            collective_id=0, has_side_effects=True, vmem_limit_bytes=40 * 2**20
        ),
        name="neck",
    )(*(pltpu.with_memory_space_constraint(a, pltpu.HBM) for a in operands))

    return tuple(
        pl.pallas_call(
            finish,
            out_shape=shapes,
            in_specs=[vmem] * 4,
            out_specs=[hbm] * 3,
            scratch_shapes=[pltpu.VMEM(s.shape, F32) for s in shapes] + [dma((3, B))],
            compiler_params=pltpu.CompilerParams(vmem_limit_bytes=16 * 2**20),
            name="finish",
        )(*filtered)
    )


def solution(mesh):
    torus = Mesh(mesh.devices.reshape(NZ, NX, NY, NC), AXES)
    strips = P("z", SPACE, None, None)
    kernels = P(None, None, None, AXES)
    return jax.shard_map(
        local,
        mesh=torus,
        in_specs=(strips,) * 3 + (kernels,) * 3 + (P(),) * 6,
        out_specs=(strips,) * 3,
        check_vma=False,
    )
```

time: 65.5 us -> 51.1 us (0.78)
  local copies, waits for them, and re-layouts: 5.11 us -> 0 us
  other arithmetic: 4.62 us -> 0 us
  Pallas kernels: 54.8 us -> 50.3 us
    unnamed x16 -> x0, local copies, waits for them, and re-layouts: 5.1 us -> none
    add x3 -> x0, other arithmetic: 4.62 us -> none  [normalize(): return deviation * scale[level][:, None, None, :] * gain + shift]
    pallas_call x1 -> x2, Pallas kernels: 54.8 us -> 50.3 us  [the longest x1 48.7 us: local(): pl.pallas_call(kernel, out_shape=shapes + [jax.ShapeDtypeStruct((3, 3, B,...]
where the time goes in v2:
time: 51.1 us; the launch traced here: 51 us
  Pallas kernels  50.3 us (98%)
  between operations  0.64 us (1%)
    pallas_call x1, Pallas kernels, local(): pl.pallas_call(kernel, out_shape=shapes + [jax.ShapeDtypeStruct((3, 3, B,...  48.7 us
    pallas_call x1, Pallas kernels, local(): pl.pallas_call(finish, out_shape=shapes, in_specs=[vmem] * 4, out_specs=[...  1.67 us

profile of v2, /device:TPU:1, one launch (start us, length us, event | category | flops | bytes accessed | tf_op | source)
XLA Modules:
  0.0 51.0 jit_solution(4192045464710536562)
XLA Ops:
  0.6 48.7 %neck.1 = (f32[4,4,128,256]{3,2,1,0:T(8,128)S(1)}, f32[4,2,64,256]{3,2,1,0:T(8,128)S(1)}, f32[4,1,32,256]{3,2,1,0:T(8,128)S(1)}, f32[3,3,4,256]{3,2,1,0:T(4,128)S(1)}) custom-call(bf16[4,4,128,256]{3,2,1,0:T(8,128)(2,1)} %lat3.1, bf16[4,2,64,256]{3,2,1,0:T(8,128)(2,1)} %lat4.1, bf16[4,1,32,256]{3,2,1,0:T(8,128)(2,1)} %lat5.1, bf16[3,3,256]{2,1,0:T(4,128)(2,1)} %bitcast.9, ...), custom_call_target="tpu_custom_call" | custom-call | tf_op jit(solution)/shard_map/neck/pallas_call | solution.py:402
  49.3 1.7 %finish.1 = (f32[4,4,128,256]{3,2,1,0:T(8,128)}, f32[4,2,64,256]{3,2,1,0:T(8,128)}, f32[4,1,32,256]{3,2,1,0:T(8,128)}) custom-call(f32[4,4,128,256]{3,2,1,0:T(8,128)S(1)} %get-tuple-element.7.f3, f32[4,2,64,256]{3,2,1,0:T(8,128)S(1)} %get-tuple-element.8.f4, f32[4,1,32,256]{3,2,1,0:T(8,128)S(1)} %get-tuple-element.9.f5, ...), custom_call_target="tpu_custom_call" | custom-call | tf_op jit(solution)/shard_map/finish/pallas_call | solution.py:440

commit v3 on v2

--- a/solution.py
+++ b/solution.py
@@ -159,10 +159,10 @@
             for kw in range(3):
                 tile = jnp.concatenate([r[kw : kw + 1] for r in rows], axis=0)
                 w_all[c, level, x, z, kh * 3 + kw] = tile.astype(BF16)
-        for part, taps in ((1, SPLIT), (0, DIRECT)):
+        for block, part in (((0, 1),), ((1, 1), (0, 0)), ((2, 1), (1, 0), (2, 0)))[level]:
             for d in (4, 3, 5, 2, 6, 1, 7):
-                ref = w_all.at[c, level, x, z, taps]
-                remote(ref, ref, z_send.at[0], z_recv.at[level, part], z_ids[d - 1])
+                ref = w_all.at[c, block, x, z, SPLIT if part else DIRECT]
+                remote(ref, ref, z_send.at[0], z_recv.at[block, part], z_ids[d - 1])
 
     def outer(image, _):
         rows5(image, 0, h5[0, image], first)
@@ -264,38 +264,37 @@
             sums[2 * level, image : image + 1] = jnp.sum(one, axis=0, keepdims=True)
             sums[2 * level + 1, image : image + 1] = jnp.sum(one * one, axis=0, keepdims=True)
 
-    after_z(0, 1)
     with jax.named_scope("s7_halo"):
         for level, held in ((2, h5), (1, h4), (0, h3)):
             all_of(held, halo_send.at[level], halo_recv.at[level]).wait_recv()
-    lax.fori_loop(0, 1, outer, 0)
+    lax.fori_loop(0, 2, outer, 0)
+    after_z(0, 1)
+    after_z(1, 1)
     after_z(0, 0)
-    lax.fori_loop(1, 2, outer, 0)
-    after_z(1, 1)
-    lax.fori_loop(2, B, outer, 0)
     after_x(0, 1)
-    after_z(1, 0)
-    after_x(0, 0)
     after_z(2, 1)
     after_x(1, 1)
+    lax.fori_loop(2, B, outer, 0)
+    after_z(1, 0)
     after_z(2, 0)
+    after_x(0, 0)
+    after_x(2, 1)
     receive_partner(0, 0)
     with jax.named_scope("conv3Aa"):
         ready(0, 0)
         lax.fori_loop(0, 2, conv3(0), 0)
-    after_x(1, 0)
+    after_y(0)
     with jax.named_scope("conv3Ab"):
         lax.fori_loop(2, B, conv3(0), 0)
-    after_y(0)
-    after_x(2, 1)
+    after_x(1, 0)
     receive_partner(0, 1)
     with jax.named_scope("conv3Ca"):
         ready(0, 1)
         lax.fori_loop(0, 2, conv3(1), 0)
-    after_x(2, 0)
     after_y(1)
     with jax.named_scope("conv3Cb"):
         lax.fori_loop(2, B, conv3(1), 0)
+    after_x(2, 0)
     receive_partner(1, 0)
     with jax.named_scope("conv4A"):
         conv_small(1, 0, x4, f4)
@@ -303,25 +302,29 @@
     receive_partner(1, 1)
     with jax.named_scope("conv4C"):
         conv_small(1, 1, x4, f4)
-    receive_partner(2, 0)
-    receive_partner(2, 1)
-    with jax.named_scope("conv5"):
-        conv_small(2, 0, x5, f5)
-        conv_small(2, 1, x5, f5)
+    for part in (0, 1):
+        receive_partner(2, part)
+        with jax.named_scope(f"conv5{part}"):
+            conv_small(2, part, x5, f5)
+
+    def terms(value):
+        high = value.astype(BF16)
+        rest = value - high.astype(F32)
+        middle = rest.astype(BF16)
+        low = (rest - middle.astype(F32)).astype(BF16)
+        return jnp.concatenate([high.astype(F32), middle.astype(F32), low.astype(F32)], axis=0).astype(BF16)
 
     channel = lax.broadcasted_iota(jnp.int32, (C, 128), 0)
     lane = lax.broadcasted_iota(jnp.int32, (C, 128), 1)
-    member = lax.shift_right_logical(channel, 3)
-
-    def selector(image):
-        return (lane == member + 32 * image).astype(F32)
-
+    member = (jnp.bitwise_and(lane, 31) == lax.shift_right_logical(channel, 3)).astype(F32).astype(BF16)
+    owner = lax.shift_right_logical(lax.broadcasted_iota(jnp.int32, (8, 128), 1), 5)
+
+    flat = jnp.concatenate([sums[:, image] for image in range(B)], axis=0)
+    grouped = jnp.dot(terms(flat), member, preferred_element_type=F32)
+    grouped = grouped[0:32] + grouped[32:64] + grouped[64:96]
     packed = jnp.zeros((8, 128), F32)
     for image in range(B):
-        packed += lax.dot_general(
-            sums[:, image], selector(image), (((1,), (0,)), ((), ())),
-            precision=lax.Precision.HIGHEST, preferred_element_type=F32,
-        )
+        packed = jnp.where(owner == image, grouped[8 * image : 8 * image + 8], packed)
     stat_a[slot] = packed
     for who in ring_ids:
         remote(stat_a.at[slot], stat_a.at[slot], stat_send.at[0], stat_recv.at[0], who)
@@ -345,11 +348,15 @@
             spreads += [mean, lax.rsqrt(spread + epsilon)]
         spreads += [jnp.zeros((2, 128), F32)]
         table = jnp.concatenate(spreads, axis=0)
+        chosen = jnp.concatenate(
+            [jnp.where(owner == image, table, 0.0) for image in range(B)], axis=0
+        )
+        wide = lax.dot_general(
+            terms(chosen), member, (((1,), (1,)), ((), ())), preferred_element_type=F32
+        )
+        wide = wide[0:32] + wide[32:64] + wide[64:96]
         for image in range(B):
-            spread_out = lax.dot_general(
-                table, selector(image), (((1,), (1,)), ((), ())),
-                precision=lax.Precision.HIGHEST, preferred_element_type=F32,
-            )
+            spread_out = wide[8 * image : 8 * image + 8]
             for level in range(3):
                 table_ref[level, 0, image : image + 1] = spread_out[2 * level : 2 * level + 1]
                 table_ref[level, 1, image : image + 1] = (

time: 51.1 us -> 48.6 us (0.951)
  Pallas kernels: 50.3 us -> 47.9 us
    pallas_call x1, Pallas kernels: 48.7 us -> 46.2 us  [local(): pl.pallas_call(kernel, out_shape=shapes + [jax.ShapeDtypeStruct((3, 3, B,...]
where the time goes in v3:
time: 48.6 us; the launch traced here: 48.5 us
  Pallas kernels  47.9 us (99%)
  between operations  0.64 us (1%)
    pallas_call x1, Pallas kernels, local(): pl.pallas_call(kernel, out_shape=shapes + [jax.ShapeDtypeStruct((3, 3, B,...  46.2 us
    pallas_call x1, Pallas kernels, local(): pl.pallas_call(finish, out_shape=shapes, in_specs=[vmem] * 4, out_specs=[...  1.67 us

profile of v3, /device:TPU:1, one launch (start us, length us, event | category | flops | bytes accessed | tf_op | source)
XLA Modules:
  0.0 48.5 jit_solution(605880347107129835)
XLA Ops:
  0.6 46.2 %neck.1 = (f32[4,4,128,256]{3,2,1,0:T(8,128)S(1)}, f32[4,2,64,256]{3,2,1,0:T(8,128)S(1)}, f32[4,1,32,256]{3,2,1,0:T(8,128)S(1)}, f32[3,3,4,256]{3,2,1,0:T(4,128)S(1)}) custom-call(bf16[4,4,128,256]{3,2,1,0:T(8,128)(2,1)} %lat3.1, bf16[4,2,64,256]{3,2,1,0:T(8,128)(2,1)} %lat4.1, bf16[4,1,32,256]{3,2,1,0:T(8,128)(2,1)} %lat5.1, bf16[3,3,256]{2,1,0:T(4,128)(2,1)} %bitcast.9, ...), custom_call_target="tpu_custom_call" | custom-call | tf_op jit(solution)/shard_map/neck/pallas_call | solution.py:409
  46.9 1.7 %finish.1 = (f32[4,4,128,256]{3,2,1,0:T(8,128)}, f32[4,2,64,256]{3,2,1,0:T(8,128)}, f32[4,1,32,256]{3,2,1,0:T(8,128)}) custom-call(f32[4,4,128,256]{3,2,1,0:T(8,128)S(1)} %get-tuple-element.7.f3, f32[4,2,64,256]{3,2,1,0:T(8,128)S(1)} %get-tuple-element.8.f4, f32[4,1,32,256]{3,2,1,0:T(8,128)S(1)} %get-tuple-element.9.f5, ...), custom_call_target="tpu_custom_call" | custom-call | tf_op jit(solution)/shard_map/finish/pallas_call | solution.py:447

commit v4 on v3

--- a/solution.py
+++ b/solution.py
@@ -106,10 +106,6 @@
             raw_send.at[0], raw_recv.at[level], partner,
         )
 
-    for level, lateral, held, lowest in ((2, lat5, h5, 0), (1, lat4, h4, 1), (0, lat3, h3, 3)):
-        remote(lateral.at[:, lowest], held.at[0], halo_send.at[level], halo_recv.at[level], next_id)
-        remote(lateral.at[:, 0], held.at[1], halo_send.at[level], halo_recv.at[level], prev_id)
-
     first = strip == 0
     last = strip == STRIPS - 1
     up5, up4 = repeat_matrix(32), repeat_matrix(64)
@@ -163,6 +159,10 @@
             for d in (4, 3, 5, 2, 6, 1, 7):
                 ref = w_all.at[c, block, x, z, SPLIT if part else DIRECT]
                 remote(ref, ref, z_send.at[0], z_recv.at[block, part], z_ids[d - 1])
+
+    for level, lateral, held, lowest in ((2, lat5, h5, 0), (1, lat4, h4, 1), (0, lat3, h3, 3)):
+        remote(lateral.at[:, lowest], held.at[0], halo_send.at[level], halo_recv.at[level], next_id)
+        remote(lateral.at[:, 0], held.at[1], halo_send.at[level], halo_recv.at[level], prev_id)
 
     def outer(image, _):
         rows5(image, 0, h5[0, image], first)
@@ -264,14 +264,14 @@
             sums[2 * level, image : image + 1] = jnp.sum(one, axis=0, keepdims=True)
             sums[2 * level + 1, image : image + 1] = jnp.sum(one * one, axis=0, keepdims=True)
 
+    after_z(0, 1)
+    after_z(1, 1)
+    after_z(0, 0)
+    after_x(0, 1)
     with jax.named_scope("s7_halo"):
         for level, held in ((2, h5), (1, h4), (0, h3)):
             all_of(held, halo_send.at[level], halo_recv.at[level]).wait_recv()
     lax.fori_loop(0, 2, outer, 0)
-    after_z(0, 1)
-    after_z(1, 1)
-    after_z(0, 0)
-    after_x(0, 1)
     after_z(2, 1)
     after_x(1, 1)
     lax.fori_loop(2, B, outer, 0)

time: 48.6 us -> 46.2 us (0.951)
  Pallas kernels: 47.9 us -> 45.5 us
    pallas_call x1, Pallas kernels: 46.2 us -> 43.8 us  [local(): pl.pallas_call(kernel, out_shape=shapes + [jax.ShapeDtypeStruct((3, 3, B,...]
where the time goes in v4:
time: 46.2 us
  Pallas kernels  45.5 us (98%)
  between operations  0.64 us (1%)
    pallas_call x1, Pallas kernels, local(): pl.pallas_call(kernel, out_shape=shapes + [jax.ShapeDtypeStruct((3, 3, B,...  43.8 us
    pallas_call x1, Pallas kernels, local(): pl.pallas_call(finish, out_shape=shapes, in_specs=[vmem] * 4, out_specs=[...  1.67 us

profile of v4, /device:TPU:1, one launch (start us, length us, event | category | flops | bytes accessed | tf_op | source)
XLA Modules:
  0.0 46.2 jit_solution(1683295012918151031)
XLA Ops:
  0.6 43.8 %neck.1 = (f32[4,4,128,256]{3,2,1,0:T(8,128)S(1)}, f32[4,2,64,256]{3,2,1,0:T(8,128)S(1)}, f32[4,1,32,256]{3,2,1,0:T(8,128)S(1)}, f32[3,3,4,256]{3,2,1,0:T(4,128)S(1)}) custom-call(bf16[4,4,128,256]{3,2,1,0:T(8,128)(2,1)} %lat3.1, bf16[4,2,64,256]{3,2,1,0:T(8,128)(2,1)} %lat4.1, bf16[4,1,32,256]{3,2,1,0:T(8,128)(2,1)} %lat5.1, bf16[3,3,256]{2,1,0:T(4,128)(2,1)} %bitcast.9, ...), custom_call_target="tpu_custom_call" | custom-call | tf_op jit(solution)/shard_map/neck/pallas_call | solution.py:409
  44.5 1.7 %finish.1 = (f32[4,4,128,256]{3,2,1,0:T(8,128)}, f32[4,2,64,256]{3,2,1,0:T(8,128)}, f32[4,1,32,256]{3,2,1,0:T(8,128)}) custom-call(f32[4,4,128,256]{3,2,1,0:T(8,128)S(1)} %get-tuple-element.7.f3, f32[4,2,64,256]{3,2,1,0:T(8,128)S(1)} %get-tuple-element.8.f4, f32[4,1,32,256]{3,2,1,0:T(8,128)S(1)} %get-tuple-element.9.f5, ...), custom_call_target="tpu_custom_call" | custom-call | tf_op jit(solution)/shard_map/finish/pallas_call | solution.py:447

commit v5 on v4

--- a/solution.py
+++ b/solution.py
@@ -14,6 +14,7 @@
 C, G, B = 256, 32, 4
 HALF = 128
 LEVELS = ((4, 128), (2, 64), (1, 32))
+DIRECT_TAPS = (3, 3, 3)
 epsilon = 1e-05
 F32, BF16 = jnp.float32, jnp.bfloat16
 
@@ -41,7 +42,7 @@
 def kernel(
     lat3, lat4, lat5, w3, w4, w5, g3, b3, g4, b4, g5, b5,
     f3, f4, f5, table_ref,
-    w_all, w_tap, raw, l3, l4, l5, h3, h4, h5, x3, x4, x5, sums, stat_a, stat_b, params,
+    w_all, w_tap, raw, l3, l4, l5, h3, h4, h5, x3, x4, x5, sums, stats, params,
     local_sem, raw_send, raw_recv, z_send, z_recv, x_send, x_recv, y_send, y_recv, c_send, c_recv,
     halo_send, halo_recv, stat_send, stat_recv,
 ):
@@ -58,6 +59,16 @@
     y_ids = [(z, x, wrap(y + d, NY), c) for d in (1, 2, 3)]
     x_ids = [(z, wrap(x + d, NX), y, c) for d in (1, 2, 3)]
     z_ids = [(wrap(z + d, NZ), x, y, c) for d in range(1, NZ)]
+
+    xs = [x] + [who[1] for who in x_ids]
+    ys = [y] + [who[2] for who in y_ids]
+    plane_ids = [
+        (z, to_x, to_y, to_c)
+        for i, to_x in enumerate(xs)
+        for j, to_y in enumerate(ys)
+        for k, to_c in enumerate((c, other))
+        if i + j + k > 0
+    ]
 
     barrier = pltpu.get_barrier_semaphore()
     greeted = z_ids + x_ids + ring_ids + [next_id, prev_id]
@@ -143,7 +154,8 @@
     with jax.named_scope("s5_own"):
         lax.fori_loop(0, B, own, 0)
 
-    DIRECT, SPLIT = slice(0, 4), slice(4, 9)
+    DIRECT = [slice(0, n) for n in DIRECT_TAPS]
+    SPLIT = [slice(n, 9) for n in DIRECT_TAPS]
     quarter = pl.ds(2 * y, 2)
     pltpu.make_async_copy(raw.at[0], raw.at[0], local_sem.at[3]).wait()
 
@@ -157,7 +169,7 @@
                 w_all[c, level, x, z, kh * 3 + kw] = tile.astype(BF16)
         for block, part in (((0, 1),), ((1, 1), (0, 0)), ((2, 1), (1, 0), (2, 0)))[level]:
             for d in (4, 3, 5, 2, 6, 1, 7):
-                ref = w_all.at[c, block, x, z, SPLIT if part else DIRECT]
+                ref = w_all.at[c, block, x, z, (SPLIT if part else DIRECT)[block]]
                 remote(ref, ref, z_send.at[0], z_recv.at[block, part], z_ids[d - 1])
 
     for level, lateral, held, lowest in ((2, lat5, h5, 0), (1, lat4, h4, 1), (0, lat3, h3, 3)):
@@ -177,7 +189,7 @@
         remote(ref, ref, c_send.at[0], c_recv.at[level, part], partner)
 
     def after_z(level, part):
-        taps = SPLIT if part else DIRECT
+        taps = (SPLIT if part else DIRECT)[level]
         with jax.named_scope(f"z{level}{part}"):
             all_of(w_all.at[c, level, x, 0:7, taps], z_send.at[0], z_recv.at[level, part]).wait_recv()
         ref = w_all.at[c, level, x, quarter, taps] if part else w_all.at[c, level, x, :, taps]
@@ -188,32 +200,32 @@
     def after_x(level, part):
         with jax.named_scope(f"x{level}{part}"):
             if part:
-                total = w_all.at[c, level, 0:3, 0:2, SPLIT]
+                total = w_all.at[c, level, 0:3, 0:2, SPLIT[level]]
             else:
-                total = w_all.at[c, level, 0:3, :, DIRECT]
+                total = w_all.at[c, level, 0:3, :, DIRECT[level]]
             all_of(total, x_send.at[part], x_recv.at[level, part]).wait_recv()
         for d in (1, 3, 2):
             where = wrap(x - d, NX)
             if part:
-                ref = w_all.at[c, level, where, quarter, SPLIT]
+                ref = w_all.at[c, level, where, quarter, SPLIT[level]]
                 for e in (2, 1, 3):
                     remote(ref, ref, y_send.at[0], y_recv.at[level], y_ids[e - 1])
             else:
-                to_partner(level, part, w_all.at[c, level, where, :, DIRECT])
+                to_partner(level, part, w_all.at[c, level, where, :, DIRECT[level]])
 
     def after_y(level):
         with jax.named_scope(f"y{level}"):
-            all_of(w_all.at[c, level, 0:3, 0:6, SPLIT], y_send.at[0], y_recv.at[level]).wait_recv()
+            all_of(w_all.at[c, level, 0:3, 0:6, SPLIT[level]], y_send.at[0], y_recv.at[level]).wait_recv()
         for d in (1, 2, 3):
-            to_partner(level, 1, w_all.at[c, level, wrap(x - d, NX), :, SPLIT])
+            to_partner(level, 1, w_all.at[c, level, wrap(x - d, NX), :, SPLIT[level]])
 
     def receive_partner(level, part):
-        taps = SPLIT if part else DIRECT
+        taps = (SPLIT if part else DIRECT)[level]
         with jax.named_scope(f"c{level}{part}"):
             all_of(w_all.at[other, level, :, :, taps], c_send.at[0], c_recv.at[level, part]).wait_recv()
 
     def ready(level, part):
-        def tap(t, _):
+        for t in range(9)[(SPLIT if part else DIRECT)[level]]:
             for half in range(2):
                 for o in range(0, 32, 2):
                     pair = [
@@ -222,47 +234,53 @@
                     w_tap[t, o * 8 : o * 8 + 16, half * HALF : (half + 1) * HALF] = jnp.concatenate(
                         pair, axis=0
                     ).astype(BF16)
-            return 0
-
-        lax.fori_loop(4 * part, 9 if part else 4, tap, 0)
-
-    def products(pick, part, start):
-        total = start
-        for t in range(9)[SPLIT if part else DIRECT]:
+
+    def products(pick, level, part):
+        total = None
+        for t in range(9)[(SPLIT if part else DIRECT)[level]]:
             term = lax.dot_general(
                 pick(t // 3, t % 3), w_tap[t], (((1,), (1,)), ((), ())), preferred_element_type=F32
             )
             total = term if total is None else total + term
         return total
 
-    def conv3(part):
-        def step(image, _):
-            total = products(
-                lambda kh, kw: x3[kw, image, kh : kh + 4].reshape(4 * 128, C),
-                part,
-                f3[image].reshape(4 * 128, C) if part else None,
-            )
-            f3[image] = total.reshape(4, 128, C)
+    def moments(level, image, parts):
+        sums[2 * level, image : image + 1] = sum(jnp.sum(p, axis=0, keepdims=True) for p in parts)
+        sums[2 * level + 1, image : image + 1] = sum(
+            jnp.sum(p * p, axis=0, keepdims=True) for p in parts
+        )
+
+    def convolve(level, part, images, source, target, step):
+        rows, width = LEVELS[level]
+        for image in images:
+            parts = []
+            for top in range(0, rows, step):
+                total = products(
+                    lambda kh, kw: source[kw, image, top + kh : top + kh + step].reshape(step * width, C),
+                    level, part,
+                )
+                if part:
+                    total = target[image, top : top + step].reshape(step * width, C) + total
+                    parts.append(total)
+                target[image, top : top + step] = total.reshape(step, width, C)
             if part:
-                sums[0, pl.ds(image, 1)] = jnp.sum(total, axis=0, keepdims=True)
-                sums[1, pl.ds(image, 1)] = jnp.sum(total * total, axis=0, keepdims=True)
-            return 0
-
-        return step
+                moments(level, image, parts)
+
+    def conv3(part, images):
+        convolve(0, part, images, x3, f3, 2)
 
     def conv_small(level, part, source, target):
         rows, width = LEVELS[level]
         ready(level, part)
+        block = B * width * rows
         total = products(
-            lambda kh, kw: source[kw, :, kh : kh + rows].reshape(B * rows * width, C),
-            part,
-            target[...].reshape(B * rows * width, C) if part else None,
-        )
+            lambda kh, kw: source[kw, :, kh : kh + rows].reshape(block, C), level, part
+        )
+        if part:
+            total = target[...].reshape(block, C) + total
+            for image in range(B):
+                moments(level, image, [total[image * rows * width : (image + 1) * rows * width]])
         target[...] = total.reshape(B, rows, width, C)
-        for image in range(B if part else 0):
-            one = total[image * rows * width : (image + 1) * rows * width]
-            sums[2 * level, image : image + 1] = jnp.sum(one, axis=0, keepdims=True)
-            sums[2 * level + 1, image : image + 1] = jnp.sum(one * one, axis=0, keepdims=True)
 
     after_z(0, 1)
     after_z(1, 1)
@@ -282,18 +300,18 @@
     receive_partner(0, 0)
     with jax.named_scope("conv3Aa"):
         ready(0, 0)
-        lax.fori_loop(0, 2, conv3(0), 0)
+        conv3(0, (0, 1))
     after_y(0)
     with jax.named_scope("conv3Ab"):
-        lax.fori_loop(2, B, conv3(0), 0)
+        conv3(0, (2, 3))
     after_x(1, 0)
     receive_partner(0, 1)
     with jax.named_scope("conv3Ca"):
         ready(0, 1)
-        lax.fori_loop(0, 2, conv3(1), 0)
+        conv3(1, (0, 1))
     after_y(1)
     with jax.named_scope("conv3Cb"):
-        lax.fori_loop(2, B, conv3(1), 0)
+        conv3(1, (2, 3))
     after_x(2, 0)
     receive_partner(1, 0)
     with jax.named_scope("conv4A"):
@@ -325,17 +343,12 @@
     packed = jnp.zeros((8, 128), F32)
     for image in range(B):
         packed = jnp.where(owner == image, grouped[8 * image : 8 * image + 8], packed)
-    stat_a[slot] = packed
-    for who in ring_ids:
-        remote(stat_a.at[slot], stat_a.at[slot], stat_send.at[0], stat_recv.at[0], who)
+    stats[strip] = packed
+    for who in plane_ids:
+        remote(stats.at[strip], stats.at[strip], stat_send.at[0], stat_recv.at[0], who)
     with jax.named_scope("u1_stat"):
-        all_of(stat_a.at[0:7], stat_send.at[0], stat_recv.at[0]).wait_recv()
-    stat_b[x] = jnp.sum(stat_a[...], axis=0)
-    for who in x_ids:
-        remote(stat_b.at[x], stat_b.at[x], stat_send.at[1], stat_recv.at[1], who)
-    with jax.named_scope("u2_stat"):
-        all_of(stat_b.at[0:3], stat_send.at[1], stat_recv.at[1]).wait_recv()
-    whole = jnp.sum(stat_b[...], axis=0)
+        all_of(stats.at[0 : STRIPS - 1], stat_send.at[0], stat_recv.at[0]).wait_recv()
+    whole = jnp.sum(stats[...], axis=0)
 
     with jax.named_scope("v1_table"):
         pltpu.make_async_copy(params, params, local_sem.at[4]).wait()
@@ -369,12 +382,13 @@
         for level, held in ((2, h5), (1, h4), (0, h3)):
             all_of(held, halo_send.at[level], halo_recv.at[level]).wait_send()
         all_of(w_all.at[c, :, 0, 0:7], z_send.at[0], z_recv.at[0, 0]).wait_send()
-        all_of(w_all.at[c, :, 0:3, :, DIRECT], x_send.at[0], x_recv.at[0, 0]).wait_send()
-        all_of(w_all.at[c, :, 0:3, 0:2, SPLIT], x_send.at[1], x_recv.at[0, 1]).wait_send()
-        all_of(w_all.at[c, :, 0:3, 0:6, SPLIT], y_send.at[0], y_recv.at[0]).wait_send()
+        for level in range(3):
+            direct, split = DIRECT[level], SPLIT[level]
+            all_of(w_all.at[c, level, 0:3, :, direct], x_send.at[0], x_recv.at[0, 0]).wait_send()
+            all_of(w_all.at[c, level, 0:3, 0:2, split], x_send.at[1], x_recv.at[0, 1]).wait_send()
+            all_of(w_all.at[c, level, 0:3, 0:6, split], y_send.at[0], y_recv.at[0]).wait_send()
         all_of(w_all.at[c], c_send.at[0], c_recv.at[0, 0]).wait_send()
-        all_of(stat_a.at[0:7], stat_send.at[0], stat_recv.at[0]).wait_send()
-        all_of(stat_b.at[0:3], stat_send.at[1], stat_recv.at[1]).wait_send()
+        all_of(stats.at[0 : STRIPS - 1], stat_send.at[0], stat_recv.at[0]).wait_send()
 
 
 def finish(f3, f4, f5, table, o3, o4, o5, s3, s4, s5, sem):
@@ -425,8 +439,7 @@
             pltpu.VMEM((3, B, 4, 64, C), BF16),
             pltpu.VMEM((3, B, 3, 32, C), BF16),
             pltpu.VMEM((8, B, C), F32),
-            pltpu.VMEM((8, 8, 128), F32),
-            pltpu.VMEM((NX, 8, 128), F32),
+            pltpu.VMEM((STRIPS, 8, 128), F32),
             pltpu.VMEM((6, 1, C), F32),
             dma((5,)),
             dma((1,)), dma((3,)),
@@ -435,7 +448,7 @@
             dma((1,)), dma((3,)),
             dma((1,)), dma((3, 2)),
             dma((3,)), dma((3,)),
-            dma((2,)), dma((2,)),
+            dma((1,)), dma((1,)),
         ],
         compiler_params=pltpu.CompilerParams(
             collective_id=0, has_side_effects=True, vmem_limit_bytes=40 * 2**20

time: 46.2 us -> 45.1 us (0.976)
  Pallas kernels: 45.5 us -> 44.4 us
    pallas_call x1, Pallas kernels: 43.8 us -> 42.7 us  [local(): pl.pallas_call(kernel, out_shape=shapes + [jax.ShapeDtypeStruct((3, 3, B,...]
where the time goes in v5:
time: 45.1 us; the launch traced here: 45 us
  Pallas kernels  44.4 us (98%)
  between operations  0.64 us (1%)
    pallas_call x1, Pallas kernels, local(): pl.pallas_call(kernel, out_shape=shapes + [jax.ShapeDtypeStruct((3, 3, B,...  42.7 us
    pallas_call x1, Pallas kernels, local(): pl.pallas_call(finish, out_shape=shapes, in_specs=[vmem] * 4, out_specs=[...  1.67 us

profile of v5, /device:TPU:1, one launch (start us, length us, event | category | flops | bytes accessed | tf_op | source)
XLA Modules:
  0.0 45.0 jit_solution(15769674758221299180)
XLA Ops:
  0.6 42.7 %neck.1 = (f32[4,4,128,256]{3,2,1,0:T(8,128)S(1)}, f32[4,2,64,256]{3,2,1,0:T(8,128)S(1)}, f32[4,1,32,256]{3,2,1,0:T(8,128)S(1)}, f32[3,3,4,256]{3,2,1,0:T(4,128)S(1)}) custom-call(bf16[4,4,128,256]{3,2,1,0:T(8,128)(2,1)} %lat3.1, bf16[4,2,64,256]{3,2,1,0:T(8,128)(2,1)} %lat4.1, bf16[4,1,32,256]{3,2,1,0:T(8,128)(2,1)} %lat5.1, bf16[3,3,256]{2,1,0:T(4,128)(2,1)} %bitcast.9, ...), custom_call_target="tpu_custom_call" | custom-call | tf_op jit(solution)/shard_map/neck/pallas_call | solution.py:423
  43.3 1.7 %finish.1 = (f32[4,4,128,256]{3,2,1,0:T(8,128)}, f32[4,2,64,256]{3,2,1,0:T(8,128)}, f32[4,1,32,256]{3,2,1,0:T(8,128)}) custom-call(f32[4,4,128,256]{3,2,1,0:T(8,128)S(1)} %get-tuple-element.7.f3, f32[4,2,64,256]{3,2,1,0:T(8,128)S(1)} %get-tuple-element.8.f4, f32[4,1,32,256]{3,2,1,0:T(8,128)S(1)} %get-tuple-element.9.f5, ...), custom_call_target="tpu_custom_call" | custom-call | tf_op jit(solution)/shard_map/finish/pallas_call | solution.py:460

commit v6 on v5

--- a/solution.py
+++ b/solution.py
@@ -64,14 +64,17 @@
     ys = [y] + [who[2] for who in y_ids]
     plane_ids = [
         (z, to_x, to_y, to_c)
-        for i, to_x in enumerate(xs)
-        for j, to_y in enumerate(ys)
-        for k, to_c in enumerate((c, other))
+        for i, j in sorted(
+            ((i, j) for i in range(4) for j in range(4)),
+            key=lambda p: abs(p[0] - 2) + abs(p[1] - 2),
+        )
+        for k in range(2)
         if i + j + k > 0
+        for to_x, to_y, to_c in ((xs[i], ys[j], (c, other)[k]),)
     ]
 
     barrier = pltpu.get_barrier_semaphore()
-    greeted = z_ids + x_ids + ring_ids + [next_id, prev_id]
+    greeted = [z_ids[d - 1] for d in (4, 3, 5, 2, 6, 1, 7)] + x_ids + [next_id, prev_id] + ring_ids
     for who in greeted:
         pl.semaphore_signal(barrier, 1, device_id=who, device_id_type=MESH)
 

time: 45.1 us -> 45 us (level)
  no operation moved by 1% of the time
where the time goes in v6:
time: 45 us; the launch traced here: 44.9 us
  Pallas kernels  44.3 us (98%)
  between operations  0.64 us (1%)
    pallas_call x1, Pallas kernels, local(): pl.pallas_call(kernel, out_shape=shapes + [jax.ShapeDtypeStruct((3, 3, B,...  42.6 us
    pallas_call x1, Pallas kernels, local(): pl.pallas_call(finish, out_shape=shapes, in_specs=[vmem] * 4, out_specs=[...  1.67 us

profile of v6, /device:TPU:1, one launch (start us, length us, event | category | flops | bytes accessed | tf_op | source)
XLA Modules:
  0.0 44.9 jit_solution(1136668397800807923)
XLA Ops:
  0.6 42.6 %neck.1 = (f32[4,4,128,256]{3,2,1,0:T(8,128)S(1)}, f32[4,2,64,256]{3,2,1,0:T(8,128)S(1)}, f32[4,1,32,256]{3,2,1,0:T(8,128)S(1)}, f32[3,3,4,256]{3,2,1,0:T(4,128)S(1)}) custom-call(bf16[4,4,128,256]{3,2,1,0:T(8,128)(2,1)} %lat3.1, bf16[4,2,64,256]{3,2,1,0:T(8,128)(2,1)} %lat4.1, bf16[4,1,32,256]{3,2,1,0:T(8,128)(2,1)} %lat5.1, bf16[3,3,256]{2,1,0:T(4,128)(2,1)} %bitcast.9, ...), custom_call_target="tpu_custom_call" | custom-call | tf_op jit(solution)/shard_map/neck/pallas_call | solution.py:426
  43.2 1.7 %finish.1 = (f32[4,4,128,256]{3,2,1,0:T(8,128)}, f32[4,2,64,256]{3,2,1,0:T(8,128)}, f32[4,1,32,256]{3,2,1,0:T(8,128)}) custom-call(f32[4,4,128,256]{3,2,1,0:T(8,128)S(1)} %get-tuple-element.7.f3, f32[4,2,64,256]{3,2,1,0:T(8,128)S(1)} %get-tuple-element.8.f4, f32[4,1,32,256]{3,2,1,0:T(8,128)S(1)} %get-tuple-element.9.f5, ...), custom_call_target="tpu_custom_call" | custom-call | tf_op jit(solution)/shard_map/finish/pallas_call | solution.py:463
